TPU v7x, 32 devices: a whole 2x2x4 slice. The times are simulated.
32 devices in a mesh: wide: 8 (over z, y), narrow: 4 (over x, core).
Axes of the slice: x: 2, y: 2, z: 4, core: 2. Of those that a mesh axis runs over, the one named last changes fastest.
Arguments:
- coords_inner: float32 [2, 8192], P(None, ('wide', 'narrow')), may hold values from -1 to 1
- velocity: float32 [2, 8192], P(None, ('wide', 'narrow')), may hold values from -6 to 6
- source: float32 [8192], P(('wide', 'narrow')), may hold values from -6 to 6
- coords_edge: float32 [2, 4096], P(None, ('wide', 'narrow')), may hold values from -1 to 1
- flux_weight: float32 [2, 4096], P(None, ('wide', 'narrow')), may hold values from -6 to 6
- owner: int32 [4096, 1], P(('wide', 'narrow')), may hold values from 0 to 7; in each aligned block of 128 rows (0 to 127, 128 to 255, ...) at most 32 rows name the same one
- local_face: int32 [4096], P(('wide', 'narrow')), may hold values from 0 to 127
- w_first: float32 [2, 512], replicated, may hold values from -4 to 4
- b_first: float32 [512], replicated, may hold values from -3 to 3
- w_hidden: float32 [4, 512, 512], replicated, may hold values from -0.25 to 0.25
- b_hidden: float32 [4, 512], replicated, may hold values from -3 to 3
- w_last: float32 [512], replicated, may hold values from -0.25 to 0.25
Outputs:
- face_integral: float32 [1024], P('wide')
- grad_first: float32 [2, 512], replicated
- grad_hidden: float32 [4, 512, 512], replicated
- grad_last: float32 [512], replicated
Inputs may be any that keep to these rules, and one draw needn't show every extreme that they name: Among the 128 face points of one device no owner appears more than 32 times, and some owner appears exactly 32 times.
All inputs are finite; a program needn't handle non-finite values.
Results may differ from a plain program's by a relative error of at most 0.0003.
Values sent between devices are 32-bit elements; how exact they have to be, the bound alone decides.
No kernel may reach another device: no remote copies, remote signals or barrier semaphores. Data moves between devices by JAX's collectives and lax.ppermute only.
A program may use at most 128 MiB of HBM per device.

v0:
```python
import functools
import math

import jax
import jax.numpy as jnp
from jax import lax
from jax.experimental import pallas as pl
from jax.experimental.pallas import tpu as pltpu
from jax.sharding import PartitionSpec as P


FACE_DEV = 128
LANES = 128
SUB = 8
AXES = ("wide", "narrow")
ROOM = {"edge": 8, "inner": 3, "backward": 11, "gather": 4}


def CHUNKS(layers):
    middle = layers // 2
    return (
        (tuple(range(layers - 1, middle - 1, -1)), (0, 1)),
        (tuple(range(middle - 1, -1, -1)), (2, 0)),
    )


F32, BF16 = jnp.float32, jnp.bfloat16
exact = lax.Precision.HIGHEST
penalty_weight = 4.0
NN = (((1,), (0,)), ((), ()))
NT = (((1,), (1,)), ((), ()))


def split(x):
    high = x.astype(BF16)
    return high, (x - high.astype(F32)).astype(BF16)


def dot(a, b, dims=NN):
    return lax.dot_general(a, b, dims, preferred_element_type=F32)


def dot3(a, b, dims=NN):
    return dot(a[0], b[0], dims) + (dot(a[0], b[1], dims) + dot(a[1], b[0], dims))


def column(row, count):
    turned = jnp.broadcast_to(row, (LANES, row.shape[1])).T
    return jnp.concatenate([turned] * (count // LANES), 1)


def stacked(hidden, slopes):
    n = hidden.shape[1]
    scale = 1.0 - hidden * hidden
    return split(hidden), split(scale * slopes[:, :n]), split(scale * slopes[:, n:])


def join(parts):
    return tuple(jnp.concatenate([p[i] for p in parts], 1) for i in (0, 1))


VMEM = pl.BlockSpec(memory_space=pltpu.VMEM)
SMEM = pl.BlockSpec(memory_space=pltpu.SMEM)
HBM = pl.BlockSpec(memory_space=pltpu.HBM)


def call(kernel, out_shape, args, in_specs=None, scratch=(), room=8, flops=0, **more):
    shapes = [a if isinstance(a, jax.ShapeDtypeStruct) else jax.ShapeDtypeStruct(a, F32) for a in out_shape]
    moved = sum(a.size * a.dtype.itemsize for a in (*args, *shapes))
    return pl.pallas_call(
        kernel,
        in_specs=in_specs or [VMEM] * len(args),
        out_specs=more.pop("out_specs", [VMEM] * len(shapes)),
        out_shape=shapes,
        scratch_shapes=list(scratch),
        compiler_params=pltpu.CompilerParams(vmem_limit_bytes=room << 20),
        cost_estimate=pl.CostEstimate(flops=flops, bytes_accessed=moved, transcendentals=0),
        **more,
    )(*args)


def opened(coords, w_first, b_first, n):
    a, b = column(w_first[0:1, :], n), column(w_first[1:2, :], n)
    pre = a * coords[0:1, :] + b * coords[1:2, :] + column(b_first, n)
    return jnp.tanh(pre), a, b


def layer(weight, bias, hidden, slopes):
    n = hidden.shape[1]
    product = dot3(weight, join(stacked(hidden, slopes)))
    return jnp.tanh(product[:, :n] + column(bias, n)), product[:, n:]


def readout(w_last, hidden, slopes):
    row = jnp.broadcast_to(w_last, (SUB, w_last.shape[1]))
    return dot3(split(row), join(stacked(hidden, slopes)))


def edge_kernel(
    where, w_hbm, coords_hbm, first_hbm, b_first_hbm, b_hbm, last_hbm, fw_hbm, owner_hbm, face_hbm,
    hs, ps, th, tl, wh, wl, out, owners,
    w, coords, first, b_first, b, last, fw, owner, face, sem, small,
):
    layers, _, _ = w.shape
    n = coords.shape[1]
    pairs = (
        (coords_hbm, coords),
        (first_hbm, first),
        (b_first_hbm, b_first),
        (b_hbm, b),
        (last_hbm, last),
        (fw_hbm, fw),
        (owner_hbm, owner),
        (face_hbm, face),
    )
    copies = [pltpu.make_async_copy(src, dst, small.at[i]) for i, (src, dst) in enumerate(pairs)]
    for copy in copies:
        copy.start()
    for k in range(layers):
        pltpu.make_async_copy(w_hbm.at[k], w.at[k], sem.at[k]).start()
    for copy in copies:
        copy.wait()
    hidden, a, c = opened(coords[...], first[...], b_first[...], n)
    hs[0] = hidden
    ps[0, :, :n] = a
    ps[0, :, n:] = c

    def body(k, carry):
        pltpu.make_async_copy(w_hbm.at[k], w.at[k], sem.at[k]).wait()
        plain = w[k]
        high, low = split(plain)
        wh[k] = high
        wl[k] = low
        high, low = split(plain.T)
        th[k] = high
        tl[k] = low
        hidden, slopes = layer((high, low), b[pl.ds(k, 1), :], hs[k], ps[k])
        hs[k + 1] = hidden
        ps[k + 1] = slopes
        return carry

    lax.fori_loop(0, layers, body, 0)
    row = readout(last[...], hs[layers], ps[layers])[0:1, :]
    flux = fw[0:1, :] * row[:, n : 2 * n] + fw[1:2, :] * row[:, 2 * n :]
    hot = (owner[...] == lax.broadcasted_iota(jnp.int32, (out.shape[0], n), 0)).astype(F32)
    owners[...] = hot
    faces = (face[...] == lax.broadcasted_iota(jnp.int32, (FACE_DEV, n), 0)).astype(F32)
    out[...] = lax.dot_general(hot * flux, faces, NT, precision=exact, preferred_element_type=F32)


def edge_forward(me, wide, w_hidden, coords, w_first, b_first, b_hidden, w_last, flux_weight, owner, face):
    layers, d, _ = w_hidden.shape
    n = coords.shape[1]
    arrays = (w_hidden, coords, w_first, b_first, b_hidden, w_last, flux_weight, owner, face)
    arrays = tuple(pltpu.with_memory_space_constraint(a, pltpu.HBM) for a in arrays)
    args = (me, *arrays)
    half = jax.ShapeDtypeStruct(w_hidden.shape, BF16)
    return call(
        edge_kernel,
        [(layers + 1, d, n), (layers + 1, d, 2 * n), half, half, half, half, (wide, FACE_DEV), (wide, n)],
        args,
        in_specs=[SMEM] + [HBM] * len(arrays),
        scratch=[pltpu.VMEM(a.shape, a.dtype) for a in arrays]
        + [pltpu.SemaphoreType.DMA((layers,)), pltpu.SemaphoreType.DMA((len(arrays) - 1,))],
        room=ROOM["edge"],
        flops=18 * layers * d * d * n,
    )


def inner_kernel(k, first, last, *refs):
    refs = list(refs)
    take = lambda count: [refs.pop(0) for _ in range(count)]
    th, tl, b = take(3)
    if first:
        coords, w_first, b_first = take(3)
    else:
        h, p = take(2)
    if last:
        (w_last,) = take(1)
    if first:
        h0, p0 = take(2)
    h1, p1 = take(2)
    if first:
        n = coords.shape[1]
        hidden, a, c = opened(coords[...], w_first[...], b_first[...], n)
        h0[...] = hidden
        p0[:, :n] = a
        p0[:, n:] = c
        slopes = jnp.concatenate([a, c], 1)
    else:
        hidden, slopes = h[...], p[...]
    hidden, slopes = layer((th[k], tl[k]), b[k : k + 1, :], hidden, slopes)
    h1[...] = hidden
    p1[...] = slopes
    if last:
        (sums,) = take(1)
        sums[...] = readout(w_last[...], hidden, slopes)


def inner_forward(k, n, weights, b_hidden, start, w_last):
    _, d, _ = weights[0].shape
    first, last = len(start) == 3, w_last is not None
    args = (*weights, b_hidden, *start) + ((w_last,) if last else ())
    shapes = [(d, n), (d, 2 * n)] * (2 if first else 1) + ([(SUB, 3 * n)] if last else [])
    return call(
        functools.partial(inner_kernel, k, first, last),
        shapes,
        args,
        room=ROOM["inner"],
        flops=18 * d * d * n,
    )


def owner_of(me, own, other, position):
    a, b = own[position], other[position]
    if a == b:
        return me ^ a
    return me ^ jnp.where(me % 2 == 0, a, b)


def scatter(me, tables, per, flat, keep, send):
    count = len(tables[0])
    half = count // 2
    for position in range(count):
        target, place_at = (keep, position) if position < half else (send, position - half)
        first = owner_of(me, *tables, position) * SUB
        for unit in range(per):
            start = pl.multiple_of(first + unit * SUB * count, SUB)
            target[place_at, unit * SUB : (unit + 1) * SUB, :] = flat[pl.ds(start, SUB), :]


def differentials(hidden, slopes, cot):
    n = hidden.shape[1]
    scale = 1.0 - hidden * hidden
    d_hidden, d_0, d_1 = cot[:, :n], cot[:, n : 2 * n], cot[:, 2 * n :]
    d_scale = d_0 * slopes[:, :n] + d_1 * slopes[:, n:]
    return scale * (d_hidden - 2.0 * hidden * d_scale), scale * d_0, scale * d_1


def backward_kernel(k, opening, closing, tables, face_scale, inner_scale, per, narrow, *refs):
    refs = list(refs)
    take = lambda count: [refs.pop(0) for _ in range(count)]
    where, wh, wl = take(3)
    h_low, p_low, h_top, p_top, hs, ps = take(6)
    if opening:
        isums, velocity, source, full, owners, face, flux_weight, w_last = take(8)
    else:
        cot_in = take(2)
    if closing:
        coords = take(2)
        (g_last,) = take(1)
    keep, send = take(2)
    if not closing:
        cot_out = take(2)
    if opening:
        g_out, integral = take(2)
        cot_in = cot_out
    if closing:
        cot_out = cot_in
        keep_more, send_more = take(2)
    xh, xl, dh, dl, flat = take(5)
    if closing:
        cot_out = take(2)
    me = where[0]
    d = wh.shape[1]
    ni, ne = h_low.shape[1], hs.shape[2]
    sizes, offsets = (ni, ne), (0, 3 * ni)
    tops = ((h_top[...], p_top[...]), (hs[k + 1], ps[k + 1]))

    if opening:
        row = isums[0:1, :]
        res = velocity[0:1, :] * row[:, ni : 2 * ni] + velocity[1:2, :] * row[:, 2 * ni :]
        res = inner_scale * (res + row[:, :ni] - source[...])
        inner = (res, res * velocity[0:1, :], res * velocity[1:2, :])
        faces = (face[...] == lax.broadcasted_iota(jnp.int32, (FACE_DEV, ne), 0)).astype(F32)
        every = full[...]
        mine = lax.broadcasted_iota(jnp.int32, every.shape, 0) == me // narrow
        integral[...] = jnp.sum(jnp.where(mine, every, 0.0), 0, keepdims=True)
        found = lax.dot_general(every, faces, NN, precision=exact, preferred_element_type=F32)
        found = face_scale * jnp.sum(owners[...] * found, 0, keepdims=True)
        edge = (jnp.zeros_like(found), found * flux_weight[0:1, :], found * flux_weight[1:2, :])
        total = None
        lift = column(w_last[...], LANES)
        for group, rows in enumerate((inner, edge)):
            n = sizes[group]
            line = jnp.concatenate(rows, 1)
            for tile in range(3 * n // LANES):
                at = slice(tile * LANES, (tile + 1) * LANES)
                cot_in[group][:, at] = lift * line[:, at]
            x = join(stacked(*tops[group]))
            part = dot3(split(jnp.broadcast_to(line, (SUB, 3 * n))), x, NT)
            total = part if total is None else total + part
        g_out[...] = total

    for group in (0, 1):
        n, at = sizes[group], offsets[group]
        for j, part in enumerate(differentials(*tops[group], cot_in[group][...])):
            high, low = split(part)
            dh[:, at + j * n : at + (j + 1) * n] = high
            dl[:, at + j * n : at + (j + 1) * n] = low
        low_level = (h_low[...], p_low[...]) if group == 0 else (hs[k], ps[k])
        for j, (high, low) in enumerate(stacked(*low_level)):
            xh[:, at + j * n : at + (j + 1) * n] = high
            xl[:, at + j * n : at + (j + 1) * n] = low

    x, delta = (xh[...], xl[...]), (dh[...], dl[...])
    grad = dot3(x, delta, NT)
    for tile in range(d // LANES):
        flat[tile * d : (tile + 1) * d, :] = grad[:, tile * LANES : (tile + 1) * LANES]
    back = dot3((wh[k], wl[k]), delta)
    cot_out[0][...] = back[:, : 3 * ni]
    cot_out[1][...] = back[:, 3 * ni :]
    scatter(me, tables, per, flat, keep, send)

    if closing:
        total = None
        for group in (0, 1):
            n = sizes[group]
            low_level = (h_low[...], p_low[...]) if group == 0 else (hs[k], ps[k])
            delta = join([split(p) for p in differentials(*low_level, cot_out[group][...])])
            one, none = jnp.ones((1, n), F32), jnp.zeros((1, n), F32)
            c = coords[group]
            rows = jnp.concatenate(
                [
                    jnp.concatenate([c[0:1, :], one, none], 1),
                    jnp.concatenate([c[1:2, :], none, one], 1),
                    jnp.zeros((SUB - 2, 3 * n), F32),
                ],
                0,
            )
            part = dot3(split(rows), delta, NT)
            total = part if total is None else total + part
        line = lambda row: [row[:, t * LANES : (t + 1) * LANES] for t in range(d // LANES)]
        rows = line(g_last[0:1, :]) + line(total[0:1, :]) + line(total[1:2, :])
        while len(rows) % SUB:
            rows.append(jnp.zeros((1, LANES), F32))
        pages = [jnp.concatenate(rows[i : i + SUB], 0) for i in range(0, len(rows), SUB)]
        half = len(tables[0]) // 2
        for position in range(2 * half):
            owner = owner_of(me, *tables, position)
            value = jnp.zeros((SUB, LANES), F32)
            for i, page in enumerate(pages):
                value = jnp.where(owner == i, page, value)
            if position < half:
                keep_more[position] = value
            else:
                send_more[position - half] = value


def backward(k, me, weights, low, top, edge, opened, carried, closed, tables, scales, narrow):
    opening, closing = opened is not None, closed is not None
    d = weights[0].shape[1]
    ni, ne = low[0].shape[1], edge[0].shape[2]
    count = len(tables[0])
    half = count // 2
    per = d * d // LANES // (SUB * count)
    args = (me, *weights, *low, *top, *edge, *(opened if opening else carried), *(closed or ()))
    shapes = [(half, per * SUB, LANES)] * 2
    if not closing:
        shapes += [(d, 3 * ni), (d, 3 * ne)]
    if opening:
        shapes += [(SUB, d), (1, FACE_DEV)]
    if closing:
        shapes += [(half, SUB, LANES)] * 2
    scratch = [pltpu.VMEM((d, 3 * (ni + ne)), BF16)] * 4 + [pltpu.VMEM((d * d // LANES, LANES), F32)]
    if closing:
        scratch += [pltpu.VMEM((d, 3 * ni), F32), pltpu.VMEM((d, 3 * ne), F32)]
    return call(
        functools.partial(backward_kernel, k, opening, closing, tables, *scales, per, narrow),
        shapes,
        args,
        in_specs=[SMEM] + [VMEM] * (len(args) - 1),
        scratch=scratch,
        room=ROOM["backward"],
        flops=36 * d * d * (ni + ne),
    )


def hop(array, pairs):
    return lax.ppermute(array, AXES, pairs)


def orders_of(count, even, odd):
    bits = [1 << i for i in range(1, count.bit_length() - 1)]

    def turned(by):
        by = by % max(1, len(bits) - 1)
        return bits[by:-1] + bits[:by] + bits[-1:]

    return turned(even), turned(odd)


def tables_of(orders):
    def offsets(order):
        found = [0]
        for bit in reversed(order):
            found = found + [bit ^ f for f in found]
        return found

    even, odd = offsets(orders[0]), offsets(orders[1])
    return tuple(even + [1 ^ f for f in odd]), tuple(odd + [1 ^ f for f in even])


def pairs_of(count, orders, stage):
    if stage == 0:
        return [(i, i ^ 1) for i in range(count)]
    return [(i, i ^ orders[i % 2][stage - 1]) for i in range(count)]


def total(count, orders, held):
    stages = count.bit_length() - 1
    for stage in range(1, stages - 1):
        middle = held.shape[0] // 2
        held = held[:middle] + hop(held[middle:], pairs_of(count, orders, stage))
    came = hop(held, pairs_of(count, orders, stages - 1))
    held = held + jnp.concatenate([came[1:], came[:1]], 0)
    for stage in range(stages - 2, 0, -1):
        held = jnp.concatenate([held, hop(held, pairs_of(count, orders, stage))], 0)
    return held, hop(held, pairs_of(count, orders, 0))


def gather_kernel(layers, tables, per, small, aliased, *refs):
    refs = list(refs)
    take = lambda count: [refs.pop(0) for _ in range(count)]
    where, *halves = take(3)
    if aliased:
        take(1)
    (out,) = take(1)
    g_first, g_last = take(2) if small else (None, None)
    buffer, sem = take(2)
    me = where[0]
    count = len(tables[0])
    d = buffer.shape[1]
    rows = SUB * count
    owners = [owner_of(me, *tables, position) for position in range(count)]
    for index, level in enumerate(layers):
        for position in range(count):
            source = halves[position // (count // 2)]
            first = owners[position] * SUB
            for unit in range(per):
                at = (index * per + unit) * SUB
                value = source[position % (count // 2), at : at + SUB, :]
                if rows <= d:
                    tile = unit * rows // d
                    start = pl.multiple_of(first + unit * rows % d, SUB)
                    buffer[index, pl.ds(start, SUB), tile * LANES : (tile + 1) * LANES] = value
                else:
                    flat = first + unit * rows
                    start = pl.multiple_of(flat % d, SUB)
                    tile = pl.multiple_of(flat // d * LANES, LANES)
                    buffer[index, pl.ds(start, SUB), pl.ds(tile, LANES)] = value
        pltpu.make_async_copy(buffer.at[index], out.at[level], sem.at[index]).start()
    if small:
        pages = [jnp.zeros((SUB, LANES), F32)] * -(-3 * d // (SUB * LANES))
        at = len(layers) * per * SUB
        for position in range(count):
            value = halves[position // (count // 2)][position % (count // 2), at : at + SUB, :]
            pages = [jnp.where(owners[position] == i, value, page) for i, page in enumerate(pages)]
        tiles = d // LANES
        for i in range(3 * tiles):
            row = pages[i // SUB][i % SUB : i % SUB + 1, :]
            lanes = slice(i % tiles * LANES, (i % tiles + 1) * LANES)
            if i < tiles:
                g_last[:, lanes] = row
            else:
                g_first[i // tiles - 1 : i // tiles, lanes] = row
    for index, level in enumerate(layers):
        pltpu.make_async_copy(buffer.at[index], out.at[level], sem.at[index]).wait()


def gather(me, shape, layers, tables, parts, before, small):
    _, d, _ = shape
    count = len(tables[0])
    per = d * d // LANES // (SUB * count)
    aliased = before is not None
    args = (me, *parts) + ((before,) if aliased else ())
    return call(
        functools.partial(gather_kernel, layers, tables, per, small, aliased),
        [shape] + ([(2, d), (1, d)] if small else []),
        args,
        in_specs=[SMEM, VMEM, VMEM] + ([HBM] if aliased else []),
        out_specs=[HBM] + ([VMEM, VMEM] if small else []),
        scratch=[pltpu.VMEM((len(layers), d, d), F32), pltpu.SemaphoreType.DMA((len(layers),))],
        room=ROOM["gather"],
        input_output_aliases={3: 0} if aliased else {},
    )


def local(
    coords_inner,
    velocity,
    source,
    coords_edge,
    flux_weight,
    owner,
    local_face,
    w_first,
    b_first,
    w_hidden,
    b_hidden,
    w_last,
):
    wide, narrow = lax.axis_size("wide"), lax.axis_size("narrow")
    count = wide * narrow
    layers, d = w_hidden.shape[:2]
    ni, ne = coords_inner.shape[1], coords_edge.shape[1]
    inner_scale = 2.0 / math.sqrt(ni * count)
    face_scale = 2.0 * penalty_weight / math.sqrt(FACE_DEV * wide)
    index = lax.axis_index("wide") * narrow + lax.axis_index("narrow")
    me = index.astype(jnp.int32)[None]
    face, owner = local_face[None], owner.reshape(1, ne)
    b_first, w_last, source = b_first[None], w_last[None], source[None]

    hs, ps, th, tl, wh, wl, full, owners = edge_forward(
        me, wide, w_hidden, coords_edge, w_first, b_first, b_hidden, w_last, flux_weight, owner, face
    )
    for bit in range(count.bit_length() - 1):
        full = full + hop(full, [(i, i ^ (1 << bit)) for i in range(count)])
    levels = []
    start = (coords_inner, w_first, b_first)
    for k in range(layers):
        found = inner_forward(k, ni, (th, tl), b_hidden, start, w_last if k == layers - 1 else None)
        if k == 0:
            levels.append(tuple(found[:2]))
            found = found[2:]
        start = tuple(found[:2])
        levels.append(start)
    isums = found[2]

    chunks = CHUNKS(layers)
    carried = None
    grad = None
    summed = []
    for layers_of, turns in chunks:
        orders = orders_of(count, *turns)
        tables = tables_of(orders)
        held = []
        for k in layers_of:
            opened = (isums, velocity, source, full, owners, face, flux_weight, w_last) if k == layers - 1 else None
            closed = (coords_inner, coords_edge, g_last) if k == 0 else None
            keep, send, *rest = backward(
                k, me, (wh, wl), levels[k], levels[k + 1], (hs, ps), opened, carried, closed, tables,
                (face_scale, inner_scale), narrow,
            )
            if opened:
                g_last, integral = rest[2:]
            if closed:
                keep, send = jnp.concatenate([keep, rest[0]], 1), jnp.concatenate([send, rest[1]], 1)
            else:
                carried = tuple(rest[:2])
            held.append(keep + hop(send, pairs_of(count, orders, 0)))
        held = held[0] if len(held) == 1 else jnp.concatenate(held, 1)
        summed.append((layers_of, tables, total(count, orders, held)))
    for layers_of, tables, parts in summed:
        found = gather(me, (layers, d, d), layers_of, tables, parts, grad, 0 in layers_of)
        grad = found[0]
        if 0 in layers_of:
            g_first, g_last = found[1:]
    return (integral.reshape(-1), g_first, grad, g_last.reshape(-1))


def solution(mesh):
    placed = (
        P(None, AXES),
        P(None, AXES),
        P(AXES),
        P(None, AXES),
        P(None, AXES),
        P(AXES, None),
        P(AXES),
        P(),
        P(),
        P(),
        P(),
        P(),
    )

    return jax.shard_map(
        local, mesh=mesh, in_specs=placed, out_specs=(P("wide"), P(), P(), P()), check_vma=False
    )
```

profile of v0, /device:TPU:0, one launch (start us, length us, event | category | flops | bytes accessed | tf_op | source)
XLA Modules:
  0.0 126.2 jit_solution(2431942017734382306)
XLA Ops:
  0.7 7.2 %shard_map.147 = (f32[5,512,128]{2,1,0:T(8,128)S(1)}, f32[5,512,256]{2,1,0:T(8,128)S(1)}, bf16[4,512,512]{2,1,0:T(8,128)(2,1)S(1)}, bf16[4,512,512]{2,1,0:T(8,12...) custom-call(s32[1]{0:T(128)} %bitcast.where.refs_0_, ...), custom_call_target="tpu_custom_call" | custom-call | flops 2415919104 | bytes 16542724 | tf_op jit(solution)/shard_map/pallas_call | solution.py:70
  9.2 2.8 %collective-permute-start.1 = (f32[8,128]{1,0:T(8,128)S(1)}, f32[8,128]{1,0:T(8,128)S(1)}, u32[]{:S(2)}, u32[]{:S(2)}) collective-permute-start(f32[8,128]{1,0:T(8,128)S(1)} %add.55), channel_id=1, source_target_pairs={{0,2},{1,3},{2,0},{3,1},{4,6},{5,7},{6,4},{7,5},{8,10},{9,11},{10,... | collective-permute-start | bytes 12296 | tf_op jit(solution)/shard_map/ppermute | solution.py:380
  12.1 1.7 %shard_map.148 = (f32[512,256]{1,0:T(8,128)S(1)}, f32[512,512]{1,0:T(8,128)S(1)}, f32[512,256]{1,0:T(8,128)S(1)}, f32[512,512]{1,0:T(8,128)S(1)}) custom-call(bf16[4,512,512]{2,1,0:T(8,128)(2,1)S(1)} %get-tuple-element.46.refs_0_, bf16[4,512,512]{2,1,0:T(8,128)(2,1)S(1)} %get-tuple-element.47.refs_1_, f32[4,512]{1,0:T(4,128)S(1)} %copy-done, ...), custom_call_target="tpu_custom_call" | custom-call | flops 1207959552 | bytes 7356416 | tf_op jit(solution)/shard_map/pallas_call | solution.py:70
  13.8 1.9 %collective-permute-start.2 = (f32[8,128]{1,0:T(8,128)S(1)}, f32[8,128]{1,0:T(8,128)S(1)}, u32[]{:S(2)}, u32[]{:S(2)}) collective-permute-start(f32[8,128]{1,0:T(8,128)S(1)} %add.56), channel_id=1, source_target_pairs={{0,4},{1,5},{2,6},{3,7},{4,0},{5,1},{6,2},{7,3},{8,12},{9,13},{10,... | collective-permute-start | bytes 12296 | tf_op jit(solution)/shard_map/ppermute | solution.py:380
  17.5 1.9 %collective-permute-start.3 = (f32[8,128]{1,0:T(8,128)S(1)}, f32[8,128]{1,0:T(8,128)S(1)}, u32[]{:S(2)}, u32[]{:S(2)}) collective-permute-start(f32[8,128]{1,0:T(8,128)S(1)} %add.57), channel_id=1, source_target_pairs={{0,8},{1,9},{2,10},{3,11},{4,12},{5,13},{6,14},{7,15},{8,0},{9,1},... | collective-permute-start | bytes 12296 | tf_op jit(solution)/shard_map/ppermute | solution.py:380
  21.1 2.9 %collective-permute-start.4 = (f32[8,128]{1,0:T(8,128)S(1)}, f32[8,128]{1,0:T(8,128)S(1)}, u32[]{:S(2)}, u32[]{:S(2)}) collective-permute-start(f32[8,128]{1,0:T(8,128)S(1)} %add.58), channel_id=1, source_target_pairs={{0,16},{1,17},{2,18},{3,19},{4,20},{5,21},{6,22},{7,23},{8,24},{9,... | collective-permute-start | bytes 12296 | tf_op jit(solution)/shard_map/ppermute | solution.py:380
  24.0 2.4 %shard_map.151 = (f32[512,256]{1,0:T(8,128)S(1)}, f32[512,512]{1,0:T(8,128)S(1)}, f32[8,768]{1,0:T(8,128)S(1)}) custom-call(bf16[4,512,512]{2,1,0:T(8,128)(2,1)S(1)} %get-tuple-element.46.refs_0_, bf16[4,512,512]{2,1,0:T(8,128)(2,1)S(1)} %get-tuple-element.47.refs_1_, f32[4,512]{1,0:T(4,128)S(1)} %copy-done, ...), custom_call_target="tpu_custom_call" | custom-call | flops 1207959552 | bytes 7374848 | tf_op jit(solution)/shard_map/pallas_call | solution.py:70
  26.4 6.4 %shard_map.152 = (f32[16,64,128]{2,1,0:T(8,128)S(1)}, f32[16,64,128]{2,1,0:T(8,128)S(1)}, f32[512,768]{1,0:T(8,128)S(1)}, f32[512,384]{1,0:T(8,128)S(1)}, f32[8,512]{1,0:T(8,128)S(1)}, /*index=5*/f32[1,128]{1,0:T(1,128)}) custom-call(s32[1]{0:T(128)} %bitcast.where.refs_0_, bf16[4,512,512]{2,1,0:T(8,128)(2,1)S(1)} %get-tuple-element.44.refs_1_, ...), custom_call_target="tpu_custom_call" | custom-call | flops 3623878656 | bytes 14736388 | tf_op jit(solution)/shard_map/pallas_call | solution.py:70
  32.9 5.2 %shard_map.153 = (f32[16,64,128]{2,1,0:T(8,128)S(1)}, f32[16,64,128]{2,1,0:T(8,128)S(1)}, f32[512,768]{1,0:T(8,128)S(1)}, f32[512,384]{1,0:T(8,128)S(1)}) custom-call(s32[1]{0:T(128)} %bitcast.where.refs_0_, bf16[4,512,512]{2,1,0:T(8,128)(2,1)S(1)} %get-tuple-element.44.refs_1_, bf16[4,512,512]{2,1,0:T(8,128)(2,1)S(1)} %get-tuple-element.45.refs_2_, ...), custom_call_target="tpu_custom_call" | custom-call | flops 3623878656 | bytes 17039364 | tf_op jit(solution)/shard_map/pallas_call | solution.py:70
  38.6 5.0 %shard_map.154 = (f32[16,64,128]{2,1,0:T(8,128)S(1)}, f32[16,64,128]{2,1,0:T(8,128)S(1)}, f32[512,768]{1,0:T(8,128)S(1)}, f32[512,384]{1,0:T(8,128)S(1)}) custom-call(s32[1]{0:T(128)} %bitcast.where.refs_0_, bf16[4,512,512]{2,1,0:T(8,128)(2,1)S(1)} %get-tuple-element.44.refs_1_, bf16[4,512,512]{2,1,0:T(8,128)(2,1)S(1)} %get-tuple-element.45.refs_2_, ...), custom_call_target="tpu_custom_call" | custom-call | flops 3623878656 | bytes 17039364 | tf_op jit(solution)/shard_map/pallas_call | solution.py:70
  43.6 7.8 %shard_map.155 = (f32[16,64,128]{2,1,0:T(8,128)S(1)}, f32[16,64,128]{2,1,0:T(8,128)S(1)}, f32[16,8,128]{2,1,0:T(8,128)S(1)}, f32[16,8,128]{2,1,0:T(8,128)S(1)}) custom-call(s32[1]{0:T(128)} %bitcast.where.refs_0_, bf16[4,512,512]{2,1,0:T(8,128)(2,1)S(1)} %get-tuple-element.44.refs_1_, bf16[4,512,512]{2,1,0:T(8,128)(2,1)S(1)} %get-tuple-element.45.refs_2_, ...), custom_call_target="tpu_custom_call" | custom-call | flops 3623878656 | bytes 14830596 | tf_op jit(solution)/shard_map/pallas_call | solution.py:70
  54.5 1.6 %collective-permute-start.7 = (f32[8,136,128]{2,1,0:T(8,128)S(1)}, f32[8,136,128]{2,1,0:T(8,128)S(1)}, u32[]{:S(2)}, u32[]{:S(2)}) collective-permute-start(f32[8,136,128]{2,1,0:T(8,128)S(1)} %pad_maximum_fusion.3), channel_id=1, source_target_pairs={{0,8},{1,3},{2,10},{3,1},{4,12},{5,7},{6,14},{7,5},{8,0},{9,11},{1... | collective-permute-start | bytes 1671176 | tf_op jit(solution)/shard_map/ppermute | solution.py:380
  56.2 9.6 %collective-permute-done.17 = f32[8,128,128]{2,1,0:T(8,128)S(1)} collective-permute-done((f32[8,128,128]{2,1,0:T(8,128)S(1)}, f32[8,128,128]{2,1,0:T(8,128)S(1)}, u32[]{:S(2)}, u32[]{:S(2)}) %collective-permute-start.17) | collective-permute-done | bytes 524320 | tf_op jit(solution)/shard_map/ppermute | solution.py:380
  69.1 5.4 %collective-permute-done.18 = f32[4,128,128]{2,1,0:T(8,128)S(1)} collective-permute-done((f32[4,128,128]{2,1,0:T(8,128)S(1)}, f32[4,128,128]{2,1,0:T(8,128)S(1)}, u32[]{:S(2)}, u32[]{:S(2)}) %collective-permute-start.18) | collective-permute-done | bytes 262176 | tf_op jit(solution)/shard_map/ppermute | solution.py:380
  74.5 1.6 %collective-permute-start.19 = (f32[2,128,128]{2,1,0:T(8,128)S(1)}, f32[2,128,128]{2,1,0:T(8,128)S(1)}, u32[]{:S(2)}, u32[]{:S(2)}) collective-permute-start(f32[2,128,128]{2,1,0:T(8,128)S(1)} %slice.77), channel_id=1, source_target_pairs={{0,8},{1,3},{2,10},{3,1},{4,12},{5,7},{6,14},{7,5},{8,0},{9,11},{1... | collective-permute-start | bytes 393224 | tf_op jit(solution)/shard_map/ppermute | solution.py:380
  76.2 1.6 %collective-permute-start.9 = (f32[2,136,128]{2,1,0:T(8,128)S(1)}, f32[2,136,128]{2,1,0:T(8,128)S(1)}, u32[]{:S(2)}, u32[]{:S(2)}) collective-permute-start(f32[2,136,128]{2,1,0:T(8,128)S(1)} %slice.69), channel_id=1, source_target_pairs={{0,4},{1,9},{2,6},{3,11},{4,0},{5,13},{6,2},{7,15},{8,12},{9,1},{1... | collective-permute-start | bytes 417800 | tf_op jit(solution)/shard_map/ppermute | solution.py:380
  77.8 4.6 %collective-permute-done.19 = f32[2,128,128]{2,1,0:T(8,128)S(1)} collective-permute-done((f32[2,128,128]{2,1,0:T(8,128)S(1)}, f32[2,128,128]{2,1,0:T(8,128)S(1)}, u32[]{:S(2)}, u32[]{:S(2)}) %collective-permute-start.19) | collective-permute-done | bytes 131104 | tf_op jit(solution)/shard_map/ppermute | solution.py:380
  83.6 1.8 %collective-permute-start.10 = (f32[2,136,128]{2,1,0:T(8,128)S(1)}, f32[2,136,128]{2,1,0:T(8,128)S(1)}, u32[]{:S(2)}, u32[]{:S(2)}) collective-permute-start(f32[2,136,128]{2,1,0:T(8,128)S(1)} %slice_add_fusion.2), channel_id=1, source_target_pairs={{0,16},{1,17},{2,18},{3,19},{4,20},{5,21},{6,22},{7,23},{8,24},{9,... | collective-permute-start | bytes 417800 | tf_op jit(solution)/shard_map/ppermute | solution.py:380
  85.5 7.9 %collective-permute-done.20 = f32[2,128,128]{2,1,0:T(8,128)S(1)} collective-permute-done((f32[2,128,128]{2,1,0:T(8,128)S(1)}, f32[2,128,128]{2,1,0:T(8,128)S(1)}, u32[]{:S(2)}, u32[]{:S(2)}) %collective-permute-start.20) | collective-permute-done | bytes 131104 | tf_op jit(solution)/shard_map/ppermute | solution.py:380
  96.0 4.3 %collective-permute-done.11 = f32[2,136,128]{2,1,0:T(8,128)S(1)} collective-permute-done((f32[2,136,128]{2,1,0:T(8,128)S(1)}, f32[2,136,128]{2,1,0:T(8,128)S(1)}, u32[]{:S(2)}, u32[]{:S(2)}) %collective-permute-start.11) | collective-permute-done | bytes 139296 | tf_op jit(solution)/shard_map/ppermute | solution.py:380
  102.9 5.5 %collective-permute-done.12 = f32[4,136,128]{2,1,0:T(8,128)S(1)} collective-permute-done((f32[4,136,128]{2,1,0:T(8,128)S(1)}, f32[4,136,128]{2,1,0:T(8,128)S(1)}, u32[]{:S(2)}, u32[]{:S(2)}) %collective-permute-start.12) | collective-permute-done | bytes 278560 | tf_op jit(solution)/shard_map/ppermute | solution.py:380
  111.1 6.9 %collective-permute-done.13 = f32[8,136,128]{2,1,0:T(8,128)S(1)} collective-permute-done((f32[8,136,128]{2,1,0:T(8,128)S(1)}, f32[8,136,128]{2,1,0:T(8,128)S(1)}, u32[]{:S(2)}, u32[]{:S(2)}) %collective-permute-start.13) | collective-permute-done | bytes 557088 | tf_op jit(solution)/shard_map/ppermute | solution.py:380
  119.3 3.1 %collective-permute-done.24.refs_2_ = f32[16,128,128]{2,1,0:T(8,128)S(1)} collective-permute-done((f32[16,128,128]{2,1,0:T(8,128)S(1)}, f32[16,128,128]{2,1,0:T(8,128)S(1)}, u32[]{:S(2)}, u32[]{:S(2)}) %collective-permute-start.24) | collective-permute-done | bytes 1048608 | tf_op jit(solution)/shard_map/ppermute | solution.py:380
  123.9 2.1 %shard_map.157 = (f32[4,512,512]{2,1,0:T(8,128)}, f32[2,512]{1,0:T(2,128)}, f32[1,512]{1,0:T(1,128)}) custom-call(s32[1]{0:T(128)} %bitcast.where.refs_0_, f32[16,136,128]{2,1,0:T(8,128)S(1)} %pad_maximum_fusion.refs_1_, f32[16,136,128]{2,1,0:T(8,128)S(1)} %collective-permute-done.14.refs_2_, ...), custom_call_target="tpu_custom_call", output_to_operand_aliasing={{0}: (3, {})} | custom-call | bytes 10622980 | tf_op jit(solution)/shard_map/pallas_call | solution.py:70
  (89 shorter events, 23.9 us)
Async XLA Ops:
  9.2 4.6 %collective-permute-start.1 = (f32[8,128]{1,0:T(8,128)S(1)}, f32[8,128]{1,0:T(8,128)S(1)}, u32[]{:S(2)}, u32[]{:S(2)}) collective-permute-start(f32[8,128]{1,0:T(8,128)S(1)} %add.55), channel_id=1, source_target_pairs={{0,2},{1,3},{2,0},{3,1},{4,6},{5,7},{6,4},{7,5},{8,10},{9,11},{10,... | collective-permute-start | bytes 12296 | tf_op jit(solution)/shard_map/ppermute | solution.py:380
  13.8 3.7 %collective-permute-start.2 = (f32[8,128]{1,0:T(8,128)S(1)}, f32[8,128]{1,0:T(8,128)S(1)}, u32[]{:S(2)}, u32[]{:S(2)}) collective-permute-start(f32[8,128]{1,0:T(8,128)S(1)} %add.56), channel_id=1, source_target_pairs={{0,4},{1,5},{2,6},{3,7},{4,0},{5,1},{6,2},{7,3},{8,12},{9,13},{10,... | collective-permute-start | bytes 12296 | tf_op jit(solution)/shard_map/ppermute | solution.py:380
  17.5 3.6 %collective-permute-start.3 = (f32[8,128]{1,0:T(8,128)S(1)}, f32[8,128]{1,0:T(8,128)S(1)}, u32[]{:S(2)}, u32[]{:S(2)}) collective-permute-start(f32[8,128]{1,0:T(8,128)S(1)} %add.57), channel_id=1, source_target_pairs={{0,8},{1,9},{2,10},{3,11},{4,12},{5,13},{6,14},{7,15},{8,0},{9,1},... | collective-permute-start | bytes 12296 | tf_op jit(solution)/shard_map/ppermute | solution.py:380
  21.1 5.3 %collective-permute-start.4 = (f32[8,128]{1,0:T(8,128)S(1)}, f32[8,128]{1,0:T(8,128)S(1)}, u32[]{:S(2)}, u32[]{:S(2)}) collective-permute-start(f32[8,128]{1,0:T(8,128)S(1)} %add.58), channel_id=1, source_target_pairs={{0,16},{1,17},{2,18},{3,19},{4,20},{5,21},{6,22},{7,23},{8,24},{9,... | collective-permute-start | bytes 12296 | tf_op jit(solution)/shard_map/ppermute | solution.py:380
  32.9 19.2 %collective-permute-start.15 = (f32[16,64,128]{2,1,0:T(8,128)S(1)}, f32[16,64,128]{2,1,0:T(8,128)S(1)}, u32[]{:S(2)}, u32[]{:S(2)}) collective-permute-start(f32[16,64,128]{2,1,0:T(8,128)S(1)} %get-tuple-element.78), channel_id=1, source_target_pairs={{0,1},{1,0},{2,3},{3,2},{4,5},{5,4},{6,7},{7,6},{8,9},{9,8},{10,11... | collective-permute-start | bytes 1572872 | tf_op jit(solution)/shard_map/ppermute | solution.py:380
  38.0 14.1 %collective-permute-start.16 = (f32[16,64,128]{2,1,0:T(8,128)S(1)}, f32[16,64,128]{2,1,0:T(8,128)S(1)}, u32[]{:S(2)}, u32[]{:S(2)}) collective-permute-start(f32[16,64,128]{2,1,0:T(8,128)S(1)} %get-tuple-element.80), channel_id=1, source_target_pairs={{0,1},{1,0},{2,3},{3,2},{4,5},{5,4},{6,7},{7,6},{8,9},{9,8},{10,11... | collective-permute-start | bytes 1572872 | tf_op jit(solution)/shard_map/ppermute | solution.py:380
  51.5 2.9 %collective-permute-start.6 = (f32[16,72,128]{2,1,0:T(8,128)S(1)}, f32[16,72,128]{2,1,0:T(8,128)S(1)}, u32[]{:S(2)}, u32[]{:S(2)}) collective-permute-start(f32[16,72,128]{2,1,0:T(8,128)S(1)} %pad_maximum_fusion.2), channel_id=1, source_target_pairs={{0,1},{1,0},{2,3},{3,2},{4,5},{5,4},{6,7},{7,6},{8,9},{9,8},{10,11... | collective-permute-start | bytes 1769480 | tf_op jit(solution)/shard_map/ppermute | solution.py:380
  51.6 2.7 %collective-permute-start.5 = (f32[16,64,128]{2,1,0:T(8,128)S(1)}, f32[16,64,128]{2,1,0:T(8,128)S(1)}, u32[]{:S(2)}, u32[]{:S(2)}) collective-permute-start(f32[16,64,128]{2,1,0:T(8,128)S(1)} %get-tuple-element.67), channel_id=1, source_target_pairs={{0,1},{1,0},{2,3},{3,2},{4,5},{5,4},{6,7},{7,6},{8,9},{9,8},{10,11... | collective-permute-start | bytes 1572872 | tf_op jit(solution)/shard_map/ppermute | solution.py:380
  52.3 13.5 %collective-permute-start.17 = (f32[8,128,128]{2,1,0:T(8,128)S(1)}, f32[8,128,128]{2,1,0:T(8,128)S(1)}, u32[]{:S(2)}, u32[]{:S(2)}) collective-permute-start(f32[8,128,128]{2,1,0:T(8,128)S(1)} %pad_maximum_fusion.5), channel_id=1, source_target_pairs={{0,2},{1,5},{2,0},{3,7},{4,6},{5,1},{6,4},{7,3},{8,10},{9,13},{10,... | collective-permute-start | bytes 1572872 | tf_op jit(solution)/shard_map/ppermute | solution.py:380
  54.5 12.9 %collective-permute-start.7 = (f32[8,136,128]{2,1,0:T(8,128)S(1)}, f32[8,136,128]{2,1,0:T(8,128)S(1)}, u32[]{:S(2)}, u32[]{:S(2)}) collective-permute-start(f32[8,136,128]{2,1,0:T(8,128)S(1)} %pad_maximum_fusion.3), channel_id=1, source_target_pairs={{0,8},{1,3},{2,10},{3,1},{4,12},{5,7},{6,14},{7,5},{8,0},{9,11},{1... | collective-permute-start | bytes 1671176 | tf_op jit(solution)/shard_map/ppermute | solution.py:380
  65.8 8.6 %collective-permute-start.18 = (f32[4,128,128]{2,1,0:T(8,128)S(1)}, f32[4,128,128]{2,1,0:T(8,128)S(1)}, u32[]{:S(2)}, u32[]{:S(2)}) collective-permute-start(f32[4,128,128]{2,1,0:T(8,128)S(1)} %slice.75), channel_id=1, source_target_pairs={{0,4},{1,9},{2,6},{3,11},{4,0},{5,13},{6,2},{7,15},{8,12},{9,1},{1... | collective-permute-start | bytes 786440 | tf_op jit(solution)/shard_map/ppermute | solution.py:380
  67.5 8.7 %collective-permute-start.8 = (f32[4,136,128]{2,1,0:T(8,128)S(1)}, f32[4,136,128]{2,1,0:T(8,128)S(1)}, u32[]{:S(2)}, u32[]{:S(2)}) collective-permute-start(f32[4,136,128]{2,1,0:T(8,128)S(1)} %slice.67), channel_id=1, source_target_pairs={{0,2},{1,5},{2,0},{3,7},{4,6},{5,1},{6,4},{7,3},{8,10},{9,13},{10,... | collective-permute-start | bytes 835592 | tf_op jit(solution)/shard_map/ppermute | solution.py:380
  74.5 7.8 %collective-permute-start.19 = (f32[2,128,128]{2,1,0:T(8,128)S(1)}, f32[2,128,128]{2,1,0:T(8,128)S(1)}, u32[]{:S(2)}, u32[]{:S(2)}) collective-permute-start(f32[2,128,128]{2,1,0:T(8,128)S(1)} %slice.77), channel_id=1, source_target_pairs={{0,8},{1,3},{2,10},{3,1},{4,12},{5,7},{6,14},{7,5},{8,0},{9,11},{1... | collective-permute-start | bytes 393224 | tf_op jit(solution)/shard_map/ppermute | solution.py:380
  76.2 7.4 %collective-permute-start.9 = (f32[2,136,128]{2,1,0:T(8,128)S(1)}, f32[2,136,128]{2,1,0:T(8,128)S(1)}, u32[]{:S(2)}, u32[]{:S(2)}) collective-permute-start(f32[2,136,128]{2,1,0:T(8,128)S(1)} %slice.69), channel_id=1, source_target_pairs={{0,4},{1,9},{2,6},{3,11},{4,0},{5,13},{6,2},{7,15},{8,12},{9,1},{1... | collective-permute-start | bytes 417800 | tf_op jit(solution)/shard_map/ppermute | solution.py:380
  82.4 11.0 %collective-permute-start.20 = (f32[2,128,128]{2,1,0:T(8,128)S(1)}, f32[2,128,128]{2,1,0:T(8,128)S(1)}, u32[]{:S(2)}, u32[]{:S(2)}) collective-permute-start(f32[2,128,128]{2,1,0:T(8,128)S(1)} %slice_add_fusion.3), channel_id=1, source_target_pairs={{0,16},{1,17},{2,18},{3,19},{4,20},{5,21},{6,22},{7,23},{8,24},{9,... | collective-permute-start | bytes 393224 | tf_op jit(solution)/shard_map/ppermute | solution.py:380
  83.6 11.2 %collective-permute-start.10 = (f32[2,136,128]{2,1,0:T(8,128)S(1)}, f32[2,136,128]{2,1,0:T(8,128)S(1)}, u32[]{:S(2)}, u32[]{:S(2)}) collective-permute-start(f32[2,136,128]{2,1,0:T(8,128)S(1)} %slice_add_fusion.2), channel_id=1, source_target_pairs={{0,16},{1,17},{2,18},{3,19},{4,20},{5,21},{6,22},{7,23},{8,24},{9,... | collective-permute-start | bytes 417800 | tf_op jit(solution)/shard_map/ppermute | solution.py:380
  94.9 5.4 %collective-permute-start.11 = (f32[2,136,128]{2,1,0:T(8,128)S(1)}, f32[2,136,128]{2,1,0:T(8,128)S(1)}, u32[]{:S(2)}, u32[]{:S(2)}) collective-permute-start(f32[2,136,128]{2,1,0:T(8,128)S(1)} %maximum_add_fusion.1), channel_id=1, source_target_pairs={{0,4},{1,9},{2,6},{3,11},{4,0},{5,13},{6,2},{7,15},{8,12},{9,1},{1... | collective-permute-start | bytes 417800 | tf_op jit(solution)/shard_map/ppermute | solution.py:380
  95.9 5.9 %collective-permute-start.21 = (f32[2,128,128]{2,1,0:T(8,128)S(1)}, f32[2,128,128]{2,1,0:T(8,128)S(1)}, u32[]{:S(2)}, u32[]{:S(2)}) collective-permute-start(f32[2,128,128]{2,1,0:T(8,128)S(1)} %maximum_add_fusion.2), channel_id=1, source_target_pairs={{0,8},{1,3},{2,10},{3,1},{4,12},{5,7},{6,14},{7,5},{8,0},{9,11},{1... | collective-permute-start | bytes 393224 | tf_op jit(solution)/shard_map/ppermute | solution.py:380
  100.3 8.1 %collective-permute-start.12 = (f32[4,136,128]{2,1,0:T(8,128)S(1)}, f32[4,136,128]{2,1,0:T(8,128)S(1)}, u32[]{:S(2)}, u32[]{:S(2)}) collective-permute-start(f32[4,136,128]{2,1,0:T(8,128)S(1)} %pad_maximum_fusion.7), channel_id=1, source_target_pairs={{0,2},{1,5},{2,0},{3,7},{4,6},{5,1},{6,4},{7,3},{8,10},{9,13},{10,... | collective-permute-start | bytes 835592 | tf_op jit(solution)/shard_map/ppermute | solution.py:380
  101.9 8.0 %collective-permute-start.22 = (f32[4,128,128]{2,1,0:T(8,128)S(1)}, f32[4,128,128]{2,1,0:T(8,128)S(1)}, u32[]{:S(2)}, u32[]{:S(2)}) collective-permute-start(f32[4,128,128]{2,1,0:T(8,128)S(1)} %pad_maximum_fusion.8), channel_id=1, source_target_pairs={{0,4},{1,9},{2,6},{3,11},{4,0},{5,13},{6,2},{7,15},{8,12},{9,1},{1... | collective-permute-start | bytes 786440 | tf_op jit(solution)/shard_map/ppermute | solution.py:380
  108.4 9.6 %collective-permute-start.13 = (f32[8,136,128]{2,1,0:T(8,128)S(1)}, f32[8,136,128]{2,1,0:T(8,128)S(1)}, u32[]{:S(2)}, u32[]{:S(2)}) collective-permute-start(f32[8,136,128]{2,1,0:T(8,128)S(1)} %pad_maximum_fusion.4), channel_id=1, source_target_pairs={{0,8},{1,3},{2,10},{3,1},{4,12},{5,7},{6,14},{7,5},{8,0},{9,11},{1... | collective-permute-start | bytes 1671176 | tf_op jit(solution)/shard_map/ppermute | solution.py:380
  109.9 9.2 %collective-permute-start.23 = (f32[8,128,128]{2,1,0:T(8,128)S(1)}, f32[8,128,128]{2,1,0:T(8,128)S(1)}, u32[]{:S(2)}, u32[]{:S(2)}) collective-permute-start(f32[8,128,128]{2,1,0:T(8,128)S(1)} %pad_maximum_fusion.6), channel_id=1, source_target_pairs={{0,2},{1,5},{2,0},{3,7},{4,6},{5,1},{6,4},{7,3},{8,10},{9,13},{10,... | collective-permute-start | bytes 1572872 | tf_op jit(solution)/shard_map/ppermute | solution.py:380
  118.1 5.8 %collective-permute-start.14 = (f32[16,136,128]{2,1,0:T(8,128)S(1)}, f32[16,136,128]{2,1,0:T(8,128)S(1)}, u32[]{:S(2)}, u32[]{:S(2)}) collective-permute-start(f32[16,136,128]{2,1,0:T(8,128)S(1)} %pad_maximum_fusion.refs_1_), channel_id=1, source_target_pairs={{0,1},{1,0},{2,3},{3,2},{4,5},{5,4},{6,7},{7,6},{8,9},{9,8},{10,11... | collective-permute-start | bytes 3342344 | tf_op jit(solution)/shard_map/ppermute | solution.py:380
  119.2 3.2 %collective-permute-start.24 = (f32[16,128,128]{2,1,0:T(8,128)S(1)}, f32[16,128,128]{2,1,0:T(8,128)S(1)}, u32[]{:S(2)}, u32[]{:S(2)}) collective-permute-start(f32[16,128,128]{2,1,0:T(8,128)S(1)} %pad_maximum_fusion.1.refs_1_), channel_id=1, source_target_pairs={{0,1},{1,0},{2,3},{3,2},{4,5},{5,4},{6,7},{7,6},{8,9},{9,8},{10,11... | collective-permute-start | bytes 3145736 | tf_op jit(solution)/shard_map/ppermute | solution.py:380
  (11 other events, 66.3 us)
where the time goes:
time: 126 us
  waiting for transfers between devices  52.8 us (42%)
  Pallas kernels  42.2 us (33%)
  starting transfers between devices  28.9 us (23%)
    ppermute x25, waiting for transfers between devices, hop(): return lax.ppermute(array, AXES, pairs)  52.8 us
    pallas_call x11, Pallas kernels, call(): pl.pallas_call(kernel, in_specs=in_specs or [VMEM] * len(args), out_specs...  42.2 us
    ppermute x25, starting transfers between devices, hop(): return lax.ppermute(array, AXES, pairs)  28.9 us
  transfers between devices with their start and end apart: 25, of which 15 were waited for; matrix products, arithmetic and copies ran while one was open for 1% of the time, Pallas kernels for 21%

commit v1 on v0

--- a/solution.py
+++ b/solution.py
@@ -16,12 +16,8 @@
 ROOM = {"edge": 8, "inner": 3, "backward": 11, "gather": 4}
 
 
-def CHUNKS(layers):
-    middle = layers // 2
-    return (
-        (tuple(range(layers - 1, middle - 1, -1)), (0, 1)),
-        (tuple(range(middle - 1, -1, -1)), (2, 0)),
-    )
+def CHUNKS():
+    return (((3, 2), (0, 1)), ((1,), (2, 0)), ((0,), (0, 1)))
 
 
 F32, BF16 = jnp.float32, jnp.bfloat16
@@ -53,10 +49,6 @@
     n = hidden.shape[1]
     scale = 1.0 - hidden * hidden
     return split(hidden), split(scale * slopes[:, :n]), split(scale * slopes[:, n:])
-
-
-def join(parts):
-    return tuple(jnp.concatenate([p[i] for p in parts], 1) for i in (0, 1))
 
 
 VMEM = pl.BlockSpec(memory_space=pltpu.VMEM)
@@ -85,20 +77,39 @@
     return jnp.tanh(pre), a, b
 
 
-def layer(weight, bias, hidden, slopes):
+def keep_inputs(hidden, slopes, high, low):
     n = hidden.shape[1]
-    product = dot3(weight, join(stacked(hidden, slopes)))
+    for j, (h, l) in enumerate(stacked(hidden, slopes)):
+        high[:, j * n : (j + 1) * n] = h
+        low[:, j * n : (j + 1) * n] = l
+
+
+def layer(weight, bias, x):
+    product = dot3(weight, x)
+    n = product.shape[1] // 3
     return jnp.tanh(product[:, :n] + column(bias, n)), product[:, n:]
 
 
 def readout(w_last, hidden, slopes):
-    row = jnp.broadcast_to(w_last, (SUB, w_last.shape[1]))
-    return dot3(split(row), join(stacked(hidden, slopes)))
+    n = hidden.shape[1]
+    weight = column(w_last, n)
+    scaled = weight * (1.0 - hidden * hidden)
+    rows = (weight * hidden, scaled * slopes[:, :n], scaled * slopes[:, n:])
+    return jnp.concatenate([jnp.sum(row, 0, keepdims=True) for row in rows], 1)
+
+
+def folded(array):
+    return sum(array[:, at : at + LANES] for at in range(LANES, array.shape[1], LANES)) + array[:, :LANES]
+
+
+def row_sums(array):
+    ones = jnp.ones((SUB, LANES), F32)
+    return lax.dot_general(ones, array, NT, precision=exact, preferred_element_type=F32)[0:1, :]
 
 
 def edge_kernel(
     where, w_hbm, coords_hbm, first_hbm, b_first_hbm, b_hbm, last_hbm, fw_hbm, owner_hbm, face_hbm,
-    hs, ps, th, tl, wh, wl, out, owners,
+    hs, ps, xh, xl, th, tl, wh, wl, out, owners,
     w, coords, first, b_first, b, last, fw, owner, face, sem, small,
 ):
     layers, _, _ = w.shape
@@ -125,7 +136,7 @@
     ps[0, :, :n] = a
     ps[0, :, n:] = c
 
-    def body(k, carry):
+    def prepare(k):
         pltpu.make_async_copy(w_hbm.at[k], w.at[k], sem.at[k]).wait()
         plain = w[k]
         high, low = split(plain)
@@ -134,13 +145,16 @@
         high, low = split(plain.T)
         th[k] = high
         tl[k] = low
-        hidden, slopes = layer((high, low), b[pl.ds(k, 1), :], hs[k], ps[k])
+
+    prepare(0)
+    for k in range(layers):
+        if k + 1 < layers:
+            prepare(k + 1)
+        keep_inputs(hs[k], ps[k], xh.at[k], xl.at[k])
+        hidden, slopes = layer((th[k], tl[k]), b[k : k + 1, :], (xh[k], xl[k]))
         hs[k + 1] = hidden
         ps[k + 1] = slopes
-        return carry
-
-    lax.fori_loop(0, layers, body, 0)
-    row = readout(last[...], hs[layers], ps[layers])[0:1, :]
+    row = readout(last[...], hs[layers], ps[layers])
     flux = fw[0:1, :] * row[:, n : 2 * n] + fw[1:2, :] * row[:, 2 * n :]
     hot = (owner[...] == lax.broadcasted_iota(jnp.int32, (out.shape[0], n), 0)).astype(F32)
     owners[...] = hot
@@ -157,7 +171,12 @@
     half = jax.ShapeDtypeStruct(w_hidden.shape, BF16)
     return call(
         edge_kernel,
-        [(layers + 1, d, n), (layers + 1, d, 2 * n), half, half, half, half, (wide, FACE_DEV), (wide, n)],
+        [
+            *((layers + 1, d, n), (layers + 1, d, 2 * n)),
+            *[jax.ShapeDtypeStruct((layers, d, 3 * n), BF16)] * 2,
+            *[half] * 4,
+            *((wide, FACE_DEV), (wide, n)),
+        ],
         args,
         in_specs=[SMEM] + [HBM] * len(arrays),
         scratch=[pltpu.VMEM(a.shape, a.dtype) for a in arrays]
@@ -179,7 +198,7 @@
         (w_last,) = take(1)
     if first:
         h0, p0 = take(2)
-    h1, p1 = take(2)
+    h1, p1, xh, xl = take(4)
     if first:
         n = coords.shape[1]
         hidden, a, c = opened(coords[...], w_first[...], b_first[...], n)
@@ -189,7 +208,8 @@
         slopes = jnp.concatenate([a, c], 1)
     else:
         hidden, slopes = h[...], p[...]
-    hidden, slopes = layer((th[k], tl[k]), b[k : k + 1, :], hidden, slopes)
+    keep_inputs(hidden, slopes, xh, xl)
+    hidden, slopes = layer((th[k], tl[k]), b[k : k + 1, :], (xh[...], xl[...]))
     h1[...] = hidden
     p1[...] = slopes
     if last:
@@ -201,7 +221,8 @@
     _, d, _ = weights[0].shape
     first, last = len(start) == 3, w_last is not None
     args = (*weights, b_hidden, *start) + ((w_last,) if last else ())
-    shapes = [(d, n), (d, 2 * n)] * (2 if first else 1) + ([(SUB, 3 * n)] if last else [])
+    shapes = [(d, n), (d, 2 * n)] * (2 if first else 1)
+    shapes += [jax.ShapeDtypeStruct((d, 3 * n), BF16)] * 2 + ([(1, 3 * n)] if last else [])
     return call(
         functools.partial(inner_kernel, k, first, last),
         shapes,
@@ -241,12 +262,13 @@
     refs = list(refs)
     take = lambda count: [refs.pop(0) for _ in range(count)]
     where, wh, wl = take(3)
-    h_low, p_low, h_top, p_top, hs, ps = take(6)
+    xh, xl, h_top, p_top, hs, ps, eh, el = take(8)
     if opening:
         isums, velocity, source, full, owners, face, flux_weight, w_last = take(8)
     else:
         cot_in = take(2)
     if closing:
+        low = take(2)
         coords = take(2)
         (g_last,) = take(1)
     keep, send = take(2)
@@ -256,19 +278,19 @@
         g_out, integral = take(2)
         cot_in = cot_out
     if closing:
-        cot_out = cot_in
         keep_more, send_more = take(2)
-    xh, xl, dh, dl, flat = take(5)
+    deltas = (take(2), take(2))
+    (flat,) = take(1)
     if closing:
         cot_out = take(2)
     me = where[0]
     d = wh.shape[1]
-    ni, ne = h_low.shape[1], hs.shape[2]
-    sizes, offsets = (ni, ne), (0, 3 * ni)
     tops = ((h_top[...], p_top[...]), (hs[k + 1], ps[k + 1]))
+    sizes = tuple(top[0].shape[1] for top in tops)
+    ni, ne = sizes
 
     if opening:
-        row = isums[0:1, :]
+        row = isums[...]
         res = velocity[0:1, :] * row[:, ni : 2 * ni] + velocity[1:2, :] * row[:, 2 * ni :]
         res = inner_scale * (res + row[:, :ni] - source[...])
         inner = (res, res * velocity[0:1, :], res * velocity[1:2, :])
@@ -287,51 +309,39 @@
             for tile in range(3 * n // LANES):
                 at = slice(tile * LANES, (tile + 1) * LANES)
                 cot_in[group][:, at] = lift * line[:, at]
-            x = join(stacked(*tops[group]))
-            part = dot3(split(jnp.broadcast_to(line, (SUB, 3 * n))), x, NT)
+            hidden, slopes = tops[group]
+            scale = 1.0 - hidden * hidden
+            terms = hidden * rows[0] + scale * (slopes[:, :n] * rows[1] + slopes[:, n:] * rows[2])
+            part = folded(terms)
             total = part if total is None else total + part
-        g_out[...] = total
+        g_out[...] = jnp.broadcast_to(row_sums(total), g_out.shape)
 
     for group in (0, 1):
-        n, at = sizes[group], offsets[group]
+        n = sizes[group]
         for j, part in enumerate(differentials(*tops[group], cot_in[group][...])):
-            high, low = split(part)
-            dh[:, at + j * n : at + (j + 1) * n] = high
-            dl[:, at + j * n : at + (j + 1) * n] = low
-        low_level = (h_low[...], p_low[...]) if group == 0 else (hs[k], ps[k])
-        for j, (high, low) in enumerate(stacked(*low_level)):
-            xh[:, at + j * n : at + (j + 1) * n] = high
-            xl[:, at + j * n : at + (j + 1) * n] = low
-
-    x, delta = (xh[...], xl[...]), (dh[...], dl[...])
-    grad = dot3(x, delta, NT)
+            high, low_part = split(part)
+            deltas[group][0][:, j * n : (j + 1) * n] = high
+            deltas[group][1][:, j * n : (j + 1) * n] = low_part
+
+    values = [(pair[0][...], pair[1][...]) for pair in deltas]
+    grad = dot3((xh[...], xl[...]), values[0], NT) + dot3((eh[k], el[k]), values[1], NT)
     for tile in range(d // LANES):
         flat[tile * d : (tile + 1) * d, :] = grad[:, tile * LANES : (tile + 1) * LANES]
-    back = dot3((wh[k], wl[k]), delta)
-    cot_out[0][...] = back[:, : 3 * ni]
-    cot_out[1][...] = back[:, 3 * ni :]
+    for group in (0, 1):
+        cot_out[group][...] = dot3((wh[k], wl[k]), values[group])
     scatter(me, tables, per, flat, keep, send)
 
     if closing:
-        total = None
+        sums = [None, None]
         for group in (0, 1):
-            n = sizes[group]
-            low_level = (h_low[...], p_low[...]) if group == 0 else (hs[k], ps[k])
-            delta = join([split(p) for p in differentials(*low_level, cot_out[group][...])])
-            one, none = jnp.ones((1, n), F32), jnp.zeros((1, n), F32)
-            c = coords[group]
-            rows = jnp.concatenate(
-                [
-                    jnp.concatenate([c[0:1, :], one, none], 1),
-                    jnp.concatenate([c[1:2, :], none, one], 1),
-                    jnp.zeros((SUB - 2, 3 * n), F32),
-                ],
-                0,
-            )
-            part = dot3(split(rows), delta, NT)
-            total = part if total is None else total + part
+            level = (low[0][...], low[1][...]) if group == 0 else (hs[k], ps[k])
+            d_pre, *d_slopes = differentials(*level, cot_out[group][...])
+            for j in (0, 1):
+                part = folded(d_pre * coords[group][j : j + 1, :] + d_slopes[j])
+                sums[j] = part if sums[j] is None else sums[j] + part
+        total = [row_sums(part) for part in sums]
         line = lambda row: [row[:, t * LANES : (t + 1) * LANES] for t in range(d // LANES)]
-        rows = line(g_last[0:1, :]) + line(total[0:1, :]) + line(total[1:2, :])
+        rows = line(g_last[0:1, :]) + line(total[0]) + line(total[1])
         while len(rows) % SUB:
             rows.append(jnp.zeros((1, LANES), F32))
         pages = [jnp.concatenate(rows[i : i + SUB], 0) for i in range(0, len(rows), SUB)]
@@ -347,14 +357,14 @@
                 send_more[position - half] = value
 
 
-def backward(k, me, weights, low, top, edge, opened, carried, closed, tables, scales, narrow):
+def backward(k, me, weights, inputs, top, edge, opened, carried, closed, tables, scales, narrow):
     opening, closing = opened is not None, closed is not None
     d = weights[0].shape[1]
-    ni, ne = low[0].shape[1], edge[0].shape[2]
+    ni, ne = top[0].shape[1], edge[0].shape[2]
     count = len(tables[0])
     half = count // 2
     per = d * d // LANES // (SUB * count)
-    args = (me, *weights, *low, *top, *edge, *(opened if opening else carried), *(closed or ()))
+    args = (me, *weights, *inputs, *top, *edge, *(opened if opening else carried), *(closed or ()))
     shapes = [(half, per * SUB, LANES)] * 2
     if not closing:
         shapes += [(d, 3 * ni), (d, 3 * ne)]
@@ -362,7 +372,8 @@
         shapes += [(SUB, d), (1, FACE_DEV)]
     if closing:
         shapes += [(half, SUB, LANES)] * 2
-    scratch = [pltpu.VMEM((d, 3 * (ni + ne)), BF16)] * 4 + [pltpu.VMEM((d * d // LANES, LANES), F32)]
+    scratch = [pltpu.VMEM((d, 3 * n), BF16) for n in (ni, ni, ne, ne)]
+    scratch += [pltpu.VMEM((d * d // LANES, LANES), F32)]
     if closing:
         scratch += [pltpu.VMEM((d, 3 * ni), F32), pltpu.VMEM((d, 3 * ne), F32)]
     return call(
@@ -511,12 +522,12 @@
     face, owner = local_face[None], owner.reshape(1, ne)
     b_first, w_last, source = b_first[None], w_last[None], source[None]
 
-    hs, ps, th, tl, wh, wl, full, owners = edge_forward(
+    hs, ps, eh, el, th, tl, wh, wl, full, owners = edge_forward(
         me, wide, w_hidden, coords_edge, w_first, b_first, b_hidden, w_last, flux_weight, owner, face
     )
     for bit in range(count.bit_length() - 1):
         full = full + hop(full, [(i, i ^ (1 << bit)) for i in range(count)])
-    levels = []
+    levels, inputs = [], []
     start = (coords_inner, w_first, b_first)
     for k in range(layers):
         found = inner_forward(k, ni, (th, tl), b_hidden, start, w_last if k == layers - 1 else None)
@@ -525,9 +536,10 @@
             found = found[2:]
         start = tuple(found[:2])
         levels.append(start)
-    isums = found[2]
-
-    chunks = CHUNKS(layers)
+        inputs.append(tuple(found[2:4]))
+    isums = found[4]
+
+    chunks = CHUNKS()
     carried = None
     grad = None
     summed = []
@@ -537,9 +549,9 @@
         held = []
         for k in layers_of:
             opened = (isums, velocity, source, full, owners, face, flux_weight, w_last) if k == layers - 1 else None
-            closed = (coords_inner, coords_edge, g_last) if k == 0 else None
+            closed = (*levels[0], coords_inner, coords_edge, g_last) if k == 0 else None
             keep, send, *rest = backward(
-                k, me, (wh, wl), levels[k], levels[k + 1], (hs, ps), opened, carried, closed, tables,
+                k, me, (wh, wl), inputs[k], levels[k + 1], (hs, ps, eh, el), opened, carried, closed, tables,
                 (face_scale, inner_scale), narrow,
             )
             if opened:

time: 126 us -> 122 us (0.968)
  waiting for transfers between devices: 52.8 us -> 36.9 us
  starting transfers between devices: 28.9 us -> 43.3 us
  Pallas kernels: 42.2 us -> 39.7 us
    ppermute x25 -> x33, waiting for transfers between devices: 52.8 us -> 36.9 us  [hop(): return lax.ppermute(array, AXES, pairs)]
    ppermute x25 -> x33, starting transfers between devices: 28.9 us -> 43.3 us  [hop(): return lax.ppermute(array, AXES, pairs)]
    pallas_call x11 -> x12, Pallas kernels: 42.2 us -> 39.7 us  [call(): pl.pallas_call(kernel, in_specs=in_specs or [VMEM] * len(args), out_specs...]
  transfers between devices with their start and end apart: 25 -> 33, of which waited for: 15 -> 19; matrix products, arithmetic and copies ran while one was open for 1% -> 1% of each run, Pallas kernels for 21% -> 12%
where the time goes in v1:
time: 122 us
  starting transfers between devices  43.3 us (35%)
  Pallas kernels  39.7 us (33%)
  waiting for transfers between devices  36.9 us (30%)
  between operations  1.24 us (1%)
    ppermute x33, starting transfers between devices, hop(): return lax.ppermute(array, AXES, pairs)  43.3 us
    pallas_call x12, Pallas kernels, call(): pl.pallas_call(kernel, in_specs=in_specs or [VMEM] * len(args), out_specs...  39.7 us
    ppermute x33, waiting for transfers between devices, hop(): return lax.ppermute(array, AXES, pairs)  36.9 us
  transfers between devices with their start and end apart: 33, of which 19 were waited for; matrix products, arithmetic and copies ran while one was open for 1% of the time, Pallas kernels for 12%

profile of v1, /device:TPU:0, one launch (start us, length us, event | category | flops | bytes accessed | tf_op | source)
XLA Modules:
  0.0 122.2 jit_solution(4326326894246121476)
XLA Ops:
  0.7 7.2 %shard_map.147 = (f32[5,512,128]{2,1,0:T(8,128)S(1)}, f32[5,512,256]{2,1,0:T(8,128)S(1)}, bf16[4,512,384]{2,1,0:T(8,128)(2,1)S(1)}, bf16[4,512,384]{2,1,0:T(8,12...) custom-call(s32[1]{0:T(128)} %bitcast.where.refs_0_, ...), custom_call_target="tpu_custom_call" | custom-call | flops 2415919104 | bytes 19688452 | tf_op jit(solution)/shard_map/pallas_call | solution.py:62
  9.3 2.8 %collective-permute-start.1 = (f32[8,128]{1,0:T(8,128)S(1)}, f32[8,128]{1,0:T(8,128)S(1)}, u32[]{:S(2)}, u32[]{:S(2)}) collective-permute-start(f32[8,128]{1,0:T(8,128)S(1)} %add.67), channel_id=1, source_target_pairs={{0,2},{1,3},{2,0},{3,1},{4,6},{5,7},{6,4},{7,5},{8,10},{9,11},{10,... | collective-permute-start | bytes 12296 | tf_op jit(solution)/shard_map/ppermute | solution.py:391
  12.1 1.7 %shard_map.148 = (f32[512,256]{1,0:T(8,128)S(1)}, f32[512,512]{1,0:T(8,128)S(1)}, f32[512,256]{1,0:T(8,128)S(1)}, f32[512,512]{1,0:T(8,128)S(1)}, bf16[512,768]{...) custom-call(bf16[4,512,512]{2,1,0:T(8,128)(2,1)S(1)} %get-tuple-element.56.refs_0_, ...), custom_call_target="tpu_custom_call" | custom-call | flops 1207959552 | bytes 8929280 | tf_op jit(solution)/shard_map/pallas_call | solution.py:62
  13.9 1.9 %collective-permute-start.2 = (f32[8,128]{1,0:T(8,128)S(1)}, f32[8,128]{1,0:T(8,128)S(1)}, u32[]{:S(2)}, u32[]{:S(2)}) collective-permute-start(f32[8,128]{1,0:T(8,128)S(1)} %add.68), channel_id=1, source_target_pairs={{0,4},{1,5},{2,6},{3,7},{4,0},{5,1},{6,2},{7,3},{8,12},{9,13},{10,... | collective-permute-start | bytes 12296 | tf_op jit(solution)/shard_map/ppermute | solution.py:391
  17.6 1.8 %collective-permute-start.3 = (f32[8,128]{1,0:T(8,128)S(1)}, f32[8,128]{1,0:T(8,128)S(1)}, u32[]{:S(2)}, u32[]{:S(2)}) collective-permute-start(f32[8,128]{1,0:T(8,128)S(1)} %add.69), channel_id=1, source_target_pairs={{0,8},{1,9},{2,10},{3,11},{4,12},{5,13},{6,14},{7,15},{8,0},{9,1},... | collective-permute-start | bytes 12296 | tf_op jit(solution)/shard_map/ppermute | solution.py:391
  21.2 2.9 %collective-permute-start.4 = (f32[8,128]{1,0:T(8,128)S(1)}, f32[8,128]{1,0:T(8,128)S(1)}, u32[]{:S(2)}, u32[]{:S(2)}) collective-permute-start(f32[8,128]{1,0:T(8,128)S(1)} %add.70), channel_id=1, source_target_pairs={{0,16},{1,17},{2,18},{3,19},{4,20},{5,21},{6,22},{7,23},{8,24},{9,... | collective-permute-start | bytes 12296 | tf_op jit(solution)/shard_map/ppermute | solution.py:391
  25.7 6.1 %shard_map.152 = (f32[16,64,128]{2,1,0:T(8,128)S(1)}, f32[16,64,128]{2,1,0:T(8,128)S(1)}, f32[512,768]{1,0:T(8,128)S(1)}, f32[512,384]{1,0:T(8,128)S(1)}, f32[8,512]{1,0:T(8,128)S(1)}, /*index=5*/f32[1,128]{1,0:T(1,128)}) custom-call(s32[1]{0:T(128)} %bitcast.where.refs_0_, bf16[4,512,512]{2,1,0:T(8,128)(2,1)S(1)} %get-tuple-element.54.refs_1_, ...), custom_call_target="tpu_custom_call" | custom-call | flops 3623878656 | bytes 17860612 | tf_op jit(solution)/shard_map/pallas_call | solution.py:62
  31.9 4.7 %shard_map.153 = (f32[16,64,128]{2,1,0:T(8,128)S(1)}, f32[16,64,128]{2,1,0:T(8,128)S(1)}, f32[512,768]{1,0:T(8,128)S(1)}, f32[512,384]{1,0:T(8,128)S(1)}) custom-call(s32[1]{0:T(128)} %bitcast.where.refs_0_, bf16[4,512,512]{2,1,0:T(8,128)(2,1)S(1)} %get-tuple-element.54.refs_1_, bf16[4,512,512]{2,1,0:T(8,128)(2,1)S(1)} %get-tuple-element.55.refs_2_, ...), custom_call_target="tpu_custom_call" | custom-call | flops 3623878656 | bytes 20185092 | tf_op jit(solution)/shard_map/pallas_call | solution.py:62
  36.6 4.7 %shard_map.154 = (f32[16,64,128]{2,1,0:T(8,128)S(1)}, f32[16,64,128]{2,1,0:T(8,128)S(1)}, f32[512,768]{1,0:T(8,128)S(1)}, f32[512,384]{1,0:T(8,128)S(1)}) custom-call(s32[1]{0:T(128)} %bitcast.where.refs_0_, bf16[4,512,512]{2,1,0:T(8,128)(2,1)S(1)} %get-tuple-element.54.refs_1_, bf16[4,512,512]{2,1,0:T(8,128)(2,1)S(1)} %get-tuple-element.55.refs_2_, ...), custom_call_target="tpu_custom_call" | custom-call | flops 3623878656 | bytes 20185092 | tf_op jit(solution)/shard_map/pallas_call | solution.py:62
  42.0 6.4 %shard_map.155 = (f32[16,64,128]{2,1,0:T(8,128)S(1)}, f32[16,64,128]{2,1,0:T(8,128)S(1)}, f32[16,8,128]{2,1,0:T(8,128)S(1)}, f32[16,8,128]{2,1,0:T(8,128)S(1)}) custom-call(s32[1]{0:T(128)} %bitcast.where.refs_0_, bf16[4,512,512]{2,1,0:T(8,128)(2,1)S(1)} %get-tuple-element.54.refs_1_, bf16[4,512,512]{2,1,0:T(8,128)(2,1)S(1)} %get-tuple-element.55.refs_2_, ...), custom_call_target="tpu_custom_call" | custom-call | flops 3623878656 | bytes 19549188 | tf_op jit(solution)/shard_map/pallas_call | solution.py:62
  49.1 1.9 %collective-permute-start.15 = (f32[8,64,128]{2,1,0:T(8,128)S(1)}, f32[8,64,128]{2,1,0:T(8,128)S(1)}, u32[]{:S(2)}, u32[]{:S(2)}) collective-permute-start(f32[8,64,128]{2,1,0:T(8,128)S(1)} %slice.105), channel_id=1, source_target_pairs={{0,8},{1,3},{2,10},{3,1},{4,12},{5,7},{6,14},{7,5},{8,0},{9,11},{1... | collective-permute-start | bytes 786440 | tf_op jit(solution)/shard_map/ppermute | solution.py:391
  52.7 2.8 %collective-permute-done.15 = f32[8,64,128]{2,1,0:T(8,128)S(1)} collective-permute-done((f32[8,64,128]{2,1,0:T(8,128)S(1)}, f32[8,64,128]{2,1,0:T(8,128)S(1)}, u32[]{:S(2)}, u32[]{:S(2)}) %collective-permute-start.15) | collective-permute-done | bytes 262176 | tf_op jit(solution)/shard_map/ppermute | solution.py:391
  55.5 1.8 %collective-permute-start.16 = (f32[4,64,128]{2,1,0:T(8,128)S(1)}, f32[4,64,128]{2,1,0:T(8,128)S(1)}, u32[]{:S(2)}, u32[]{:S(2)}) collective-permute-start(f32[4,64,128]{2,1,0:T(8,128)S(1)} %slice.107), channel_id=1, source_target_pairs={{0,2},{1,5},{2,0},{3,7},{4,6},{5,1},{6,4},{7,3},{8,10},{9,13},{10,... | collective-permute-start | bytes 393224 | tf_op jit(solution)/shard_map/ppermute | solution.py:391
  57.8 4.0 %collective-permute-done.16 = f32[4,64,128]{2,1,0:T(8,128)S(1)} collective-permute-done((f32[4,64,128]{2,1,0:T(8,128)S(1)}, f32[4,64,128]{2,1,0:T(8,128)S(1)}, u32[]{:S(2)}, u32[]{:S(2)}) %collective-permute-start.16) | collective-permute-done | bytes 131104 | tf_op jit(solution)/shard_map/ppermute | solution.py:391
  66.7 2.6 %collective-permute-start.18 = (f32[2,64,128]{2,1,0:T(8,128)S(1)}, f32[2,64,128]{2,1,0:T(8,128)S(1)}, u32[]{:S(2)}, u32[]{:S(2)}) collective-permute-start(f32[2,64,128]{2,1,0:T(8,128)S(1)} %slice_add_fusion.7), channel_id=1, source_target_pairs={{0,16},{1,17},{2,18},{3,19},{4,20},{5,21},{6,22},{7,23},{8,24},{9,... | collective-permute-start | bytes 196616 | tf_op jit(solution)/shard_map/ppermute | solution.py:391
  73.3 1.8 %collective-permute-done.27 = f32[2,128,128]{2,1,0:T(8,128)S(1)} collective-permute-done((f32[2,128,128]{2,1,0:T(8,128)S(1)}, f32[2,128,128]{2,1,0:T(8,128)S(1)}, u32[]{:S(2)}, u32[]{:S(2)}) %collective-permute-start.27) | collective-permute-done | bytes 131104 | tf_op jit(solution)/shard_map/ppermute | solution.py:391
  75.2 3.9 %collective-permute-start.28 = (f32[2,128,128]{2,1,0:T(8,128)S(1)}, f32[2,128,128]{2,1,0:T(8,128)S(1)}, u32[]{:S(2)}, u32[]{:S(2)}) collective-permute-start(f32[2,128,128]{2,1,0:T(8,128)S(1)} %slice_add_fusion.4), channel_id=1, source_target_pairs={{0,16},{1,17},{2,18},{3,19},{4,20},{5,21},{6,22},{7,23},{8,24},{9,... | collective-permute-start | bytes 393224 | tf_op jit(solution)/shard_map/ppermute | solution.py:391
  79.0 5.3 %collective-permute-done.28 = f32[2,128,128]{2,1,0:T(8,128)S(1)} collective-permute-done((f32[2,128,128]{2,1,0:T(8,128)S(1)}, f32[2,128,128]{2,1,0:T(8,128)S(1)}, u32[]{:S(2)}, u32[]{:S(2)}) %collective-permute-start.28) | collective-permute-done | bytes 131104 | tf_op jit(solution)/shard_map/ppermute | solution.py:391
  86.1 3.5 %collective-permute-start.9 = (f32[2,72,128]{2,1,0:T(8,128)S(1)}, f32[2,72,128]{2,1,0:T(8,128)S(1)}, u32[]{:S(2)}, u32[]{:S(2)}) collective-permute-start(f32[2,72,128]{2,1,0:T(8,128)S(1)} %slice_add_fusion.6), channel_id=1, source_target_pairs={{0,16},{1,17},{2,18},{3,19},{4,20},{5,21},{6,22},{7,23},{8,24},{9,... | collective-permute-start | bytes 221192 | tf_op jit(solution)/shard_map/ppermute | solution.py:391
  89.8 2.2 %collective-permute-done.9 = f32[2,72,128]{2,1,0:T(8,128)S(1)} collective-permute-done((f32[2,72,128]{2,1,0:T(8,128)S(1)}, f32[2,72,128]{2,1,0:T(8,128)S(1)}, u32[]{:S(2)}, u32[]{:S(2)}) %collective-permute-start.9) | collective-permute-done | bytes 73760 | tf_op jit(solution)/shard_map/ppermute | solution.py:391
  93.4 5.5 %collective-permute-done.30 = f32[4,128,128]{2,1,0:T(8,128)S(1)} collective-permute-done((f32[4,128,128]{2,1,0:T(8,128)S(1)}, f32[4,128,128]{2,1,0:T(8,128)S(1)}, u32[]{:S(2)}, u32[]{:S(2)}) %collective-permute-start.30) | collective-permute-done | bytes 262176 | tf_op jit(solution)/shard_map/ppermute | solution.py:391
  102.4 2.9 %collective-permute-done.19 = f32[2,64,128]{2,1,0:T(8,128)S(1)} collective-permute-done((f32[2,64,128]{2,1,0:T(8,128)S(1)}, f32[2,64,128]{2,1,0:T(8,128)S(1)}, u32[]{:S(2)}, u32[]{:S(2)}) %collective-permute-start.19) | collective-permute-done | bytes 65568 | tf_op jit(solution)/shard_map/ppermute | solution.py:391
  108.4 1.9 %collective-permute-done.20 = f32[4,64,128]{2,1,0:T(8,128)S(1)} collective-permute-done((f32[4,64,128]{2,1,0:T(8,128)S(1)}, f32[4,64,128]{2,1,0:T(8,128)S(1)}, u32[]{:S(2)}, u32[]{:S(2)}) %collective-permute-start.20) | collective-permute-done | bytes 131104 | tf_op jit(solution)/shard_map/ppermute | solution.py:391
  111.1 5.2 %collective-permute-done.12 = f32[8,72,128]{2,1,0:T(8,128)S(1)} collective-permute-done((f32[8,72,128]{2,1,0:T(8,128)S(1)}, f32[8,72,128]{2,1,0:T(8,128)S(1)}, u32[]{:S(2)}, u32[]{:S(2)}) %collective-permute-start.12) | collective-permute-done | bytes 294944 | tf_op jit(solution)/shard_map/ppermute | solution.py:391
  (117 shorter events, 35.3 us)
Async XLA Ops:
  41.4 7.6 %collective-permute-start.14 = (f32[16,64,128]{2,1,0:T(8,128)S(1)}, f32[16,64,128]{2,1,0:T(8,128)S(1)}, u32[]{:S(2)}, u32[]{:S(2)}) collective-permute-start(f32[16,64,128]{2,1,0:T(8,128)S(1)} %get-tuple-element.96), channel_id=1, source_target_pairs={{0,1},{1,0},{2,3},{3,2},{4,5},{5,4},{6,7},{7,6},{8,9},{9,8},{10,11... | collective-permute-start | bytes 1572872 | tf_op jit(solution)/shard_map/ppermute | solution.py:391
  41.4 9.6 %collective-permute-start.24 = (f32[16,64,128]{2,1,0:T(8,128)S(1)}, f32[16,64,128]{2,1,0:T(8,128)S(1)}, u32[]{:S(2)}, u32[]{:S(2)}) collective-permute-start(f32[16,64,128]{2,1,0:T(8,128)S(1)} %get-tuple-element.100), channel_id=1, source_target_pairs={{0,1},{1,0},{2,3},{3,2},{4,5},{5,4},{6,7},{7,6},{8,9},{9,8},{10,11... | collective-permute-start | bytes 1572872 | tf_op jit(solution)/shard_map/ppermute | solution.py:391
  41.9 9.1 %collective-permute-start.23 = (f32[16,64,128]{2,1,0:T(8,128)S(1)}, f32[16,64,128]{2,1,0:T(8,128)S(1)}, u32[]{:S(2)}, u32[]{:S(2)}) collective-permute-start(f32[16,64,128]{2,1,0:T(8,128)S(1)} %get-tuple-element.98), channel_id=1, source_target_pairs={{0,1},{1,0},{2,3},{3,2},{4,5},{5,4},{6,7},{7,6},{8,9},{9,8},{10,11... | collective-permute-start | bytes 1572872 | tf_op jit(solution)/shard_map/ppermute | solution.py:391
  48.5 8.9 %collective-permute-start.5 = (f32[16,72,128]{2,1,0:T(8,128)S(1)}, f32[16,72,128]{2,1,0:T(8,128)S(1)}, u32[]{:S(2)}, u32[]{:S(2)}) collective-permute-start(f32[16,72,128]{2,1,0:T(8,128)S(1)} %pad_maximum_fusion.1), channel_id=1, source_target_pairs={{0,1},{1,0},{2,3},{3,2},{4,5},{5,4},{6,7},{7,6},{8,9},{9,8},{10,11... | collective-permute-start | bytes 1769480 | tf_op jit(solution)/shard_map/ppermute | solution.py:391
  49.1 6.4 %collective-permute-start.15 = (f32[8,64,128]{2,1,0:T(8,128)S(1)}, f32[8,64,128]{2,1,0:T(8,128)S(1)}, u32[]{:S(2)}, u32[]{:S(2)}) collective-permute-start(f32[8,64,128]{2,1,0:T(8,128)S(1)} %slice.105), channel_id=1, source_target_pairs={{0,8},{1,3},{2,10},{3,1},{4,12},{5,7},{6,14},{7,5},{8,0},{9,11},{1... | collective-permute-start | bytes 786440 | tf_op jit(solution)/shard_map/ppermute | solution.py:391
  51.2 12.4 %collective-permute-start.25 = (f32[8,128,128]{2,1,0:T(8,128)S(1)}, f32[8,128,128]{2,1,0:T(8,128)S(1)}, u32[]{:S(2)}, u32[]{:S(2)}) collective-permute-start(f32[8,128,128]{2,1,0:T(8,128)S(1)} %pad_maximum_fusion.3), channel_id=1, source_target_pairs={{0,2},{1,5},{2,0},{3,7},{4,6},{5,1},{6,4},{7,3},{8,10},{9,13},{10,... | collective-permute-start | bytes 1572872 | tf_op jit(solution)/shard_map/ppermute | solution.py:391
  55.5 6.3 %collective-permute-start.16 = (f32[4,64,128]{2,1,0:T(8,128)S(1)}, f32[4,64,128]{2,1,0:T(8,128)S(1)}, u32[]{:S(2)}, u32[]{:S(2)}) collective-permute-start(f32[4,64,128]{2,1,0:T(8,128)S(1)} %slice.107), channel_id=1, source_target_pairs={{0,2},{1,5},{2,0},{3,7},{4,6},{5,1},{6,4},{7,3},{8,10},{9,13},{10,... | collective-permute-start | bytes 393224 | tf_op jit(solution)/shard_map/ppermute | solution.py:391
  57.5 7.5 %collective-permute-start.6 = (f32[8,72,128]{2,1,0:T(8,128)S(1)}, f32[8,72,128]{2,1,0:T(8,128)S(1)}, u32[]{:S(2)}, u32[]{:S(2)}) collective-permute-start(f32[8,72,128]{2,1,0:T(8,128)S(1)} %slice.97), channel_id=1, source_target_pairs={{0,2},{1,5},{2,0},{3,7},{4,6},{5,1},{6,4},{7,3},{8,10},{9,13},{10,... | collective-permute-start | bytes 884744 | tf_op jit(solution)/shard_map/ppermute | solution.py:391
  63.6 6.4 %collective-permute-start.26 = (f32[4,128,128]{2,1,0:T(8,128)S(1)}, f32[4,128,128]{2,1,0:T(8,128)S(1)}, u32[]{:S(2)}, u32[]{:S(2)}) collective-permute-start(f32[4,128,128]{2,1,0:T(8,128)S(1)} %slice.115), channel_id=1, source_target_pairs={{0,4},{1,9},{2,6},{3,11},{4,0},{5,13},{6,2},{7,15},{8,12},{9,1},{1... | collective-permute-start | bytes 786440 | tf_op jit(solution)/shard_map/ppermute | solution.py:391
  65.0 6.7 %collective-permute-start.7 = (f32[4,72,128]{2,1,0:T(8,128)S(1)}, f32[4,72,128]{2,1,0:T(8,128)S(1)}, u32[]{:S(2)}, u32[]{:S(2)}) collective-permute-start(f32[4,72,128]{2,1,0:T(8,128)S(1)} %slice.99), channel_id=1, source_target_pairs={{0,4},{1,9},{2,6},{3,11},{4,0},{5,13},{6,2},{7,15},{8,12},{9,1},{1... | collective-permute-start | bytes 442376 | tf_op jit(solution)/shard_map/ppermute | solution.py:391
  66.7 12.3 %collective-permute-start.18 = (f32[2,64,128]{2,1,0:T(8,128)S(1)}, f32[2,64,128]{2,1,0:T(8,128)S(1)}, u32[]{:S(2)}, u32[]{:S(2)}) collective-permute-start(f32[2,64,128]{2,1,0:T(8,128)S(1)} %slice_add_fusion.7), channel_id=1, source_target_pairs={{0,16},{1,17},{2,18},{3,19},{4,20},{5,21},{6,22},{7,23},{8,24},{9,... | collective-permute-start | bytes 196616 | tf_op jit(solution)/shard_map/ppermute | solution.py:391
  70.1 5.0 %collective-permute-start.27 = (f32[2,128,128]{2,1,0:T(8,128)S(1)}, f32[2,128,128]{2,1,0:T(8,128)S(1)}, u32[]{:S(2)}, u32[]{:S(2)}) collective-permute-start(f32[2,128,128]{2,1,0:T(8,128)S(1)} %slice.117), channel_id=1, source_target_pairs={{0,8},{1,3},{2,10},{3,1},{4,12},{5,7},{6,14},{7,5},{8,0},{9,11},{1... | collective-permute-start | bytes 393224 | tf_op jit(solution)/shard_map/ppermute | solution.py:391
  71.8 14.3 %collective-permute-start.8 = (f32[2,72,128]{2,1,0:T(8,128)S(1)}, f32[2,72,128]{2,1,0:T(8,128)S(1)}, u32[]{:S(2)}, u32[]{:S(2)}) collective-permute-start(f32[2,72,128]{2,1,0:T(8,128)S(1)} %slice.101), channel_id=1, source_target_pairs={{0,8},{1,3},{2,10},{3,1},{4,12},{5,7},{6,14},{7,5},{8,0},{9,11},{1... | collective-permute-start | bytes 221192 | tf_op jit(solution)/shard_map/ppermute | solution.py:391
  75.2 9.2 %collective-permute-start.28 = (f32[2,128,128]{2,1,0:T(8,128)S(1)}, f32[2,128,128]{2,1,0:T(8,128)S(1)}, u32[]{:S(2)}, u32[]{:S(2)}) collective-permute-start(f32[2,128,128]{2,1,0:T(8,128)S(1)} %slice_add_fusion.4), channel_id=1, source_target_pairs={{0,16},{1,17},{2,18},{3,19},{4,20},{5,21},{6,22},{7,23},{8,24},{9,... | collective-permute-start | bytes 393224 | tf_op jit(solution)/shard_map/ppermute | solution.py:391
  84.4 5.3 %collective-permute-start.29 = (f32[2,128,128]{2,1,0:T(8,128)S(1)}, f32[2,128,128]{2,1,0:T(8,128)S(1)}, u32[]{:S(2)}, u32[]{:S(2)}) collective-permute-start(f32[2,128,128]{2,1,0:T(8,128)S(1)} %maximum_add_fusion.1), channel_id=1, source_target_pairs={{0,8},{1,3},{2,10},{3,1},{4,12},{5,7},{6,14},{7,5},{8,0},{9,11},{1... | collective-permute-start | bytes 393224 | tf_op jit(solution)/shard_map/ppermute | solution.py:391
  86.1 5.9 %collective-permute-start.9 = (f32[2,72,128]{2,1,0:T(8,128)S(1)}, f32[2,72,128]{2,1,0:T(8,128)S(1)}, u32[]{:S(2)}, u32[]{:S(2)}) collective-permute-start(f32[2,72,128]{2,1,0:T(8,128)S(1)} %slice_add_fusion.6), channel_id=1, source_target_pairs={{0,16},{1,17},{2,18},{3,19},{4,20},{5,21},{6,22},{7,23},{8,24},{9,... | collective-permute-start | bytes 221192 | tf_op jit(solution)/shard_map/ppermute | solution.py:391
  89.7 9.2 %collective-permute-start.30 = (f32[4,128,128]{2,1,0:T(8,128)S(1)}, f32[4,128,128]{2,1,0:T(8,128)S(1)}, u32[]{:S(2)}, u32[]{:S(2)}) collective-permute-start(f32[4,128,128]{2,1,0:T(8,128)S(1)} %pad_maximum_fusion.8), channel_id=1, source_target_pairs={{0,4},{1,9},{2,6},{3,11},{4,0},{5,13},{6,2},{7,15},{8,12},{9,1},{1... | collective-permute-start | bytes 786440 | tf_op jit(solution)/shard_map/ppermute | solution.py:391
  92.0 8.8 %collective-permute-start.10 = (f32[2,72,128]{2,1,0:T(8,128)S(1)}, f32[2,72,128]{2,1,0:T(8,128)S(1)}, u32[]{:S(2)}, u32[]{:S(2)}) collective-permute-start(f32[2,72,128]{2,1,0:T(8,128)S(1)} %maximum_add_fusion.2), channel_id=1, source_target_pairs={{0,8},{1,3},{2,10},{3,1},{4,12},{5,7},{6,14},{7,5},{8,0},{9,11},{1... | collective-permute-start | bytes 221192 | tf_op jit(solution)/shard_map/ppermute | solution.py:391
  98.9 9.2 %collective-permute-start.31 = (f32[8,128,128]{2,1,0:T(8,128)S(1)}, f32[8,128,128]{2,1,0:T(8,128)S(1)}, u32[]{:S(2)}, u32[]{:S(2)}) collective-permute-start(f32[8,128,128]{2,1,0:T(8,128)S(1)} %pad_maximum_fusion.5), channel_id=1, source_target_pairs={{0,2},{1,5},{2,0},{3,7},{4,6},{5,1},{6,4},{7,3},{8,10},{9,13},{10,... | collective-permute-start | bytes 1572872 | tf_op jit(solution)/shard_map/ppermute | solution.py:391
  100.8 6.3 %collective-permute-start.11 = (f32[4,72,128]{2,1,0:T(8,128)S(1)}, f32[4,72,128]{2,1,0:T(8,128)S(1)}, u32[]{:S(2)}, u32[]{:S(2)}) collective-permute-start(f32[4,72,128]{2,1,0:T(8,128)S(1)} %pad_maximum_fusion.9), channel_id=1, source_target_pairs={{0,4},{1,9},{2,6},{3,11},{4,0},{5,13},{6,2},{7,15},{8,12},{9,1},{1... | collective-permute-start | bytes 442376 | tf_op jit(solution)/shard_map/ppermute | solution.py:391
  105.3 5.0 %collective-permute-start.20 = (f32[4,64,128]{2,1,0:T(8,128)S(1)}, f32[4,64,128]{2,1,0:T(8,128)S(1)}, u32[]{:S(2)}, u32[]{:S(2)}) collective-permute-start(f32[4,64,128]{2,1,0:T(8,128)S(1)} %pad_maximum_fusion.10), channel_id=1, source_target_pairs={{0,2},{1,5},{2,0},{3,7},{4,6},{5,1},{6,4},{7,3},{8,10},{9,13},{10,... | collective-permute-start | bytes 393224 | tf_op jit(solution)/shard_map/ppermute | solution.py:391
  107.1 9.2 %collective-permute-start.12 = (f32[8,72,128]{2,1,0:T(8,128)S(1)}, f32[8,72,128]{2,1,0:T(8,128)S(1)}, u32[]{:S(2)}, u32[]{:S(2)}) collective-permute-start(f32[8,72,128]{2,1,0:T(8,128)S(1)} %pad_maximum_fusion.6), channel_id=1, source_target_pairs={{0,2},{1,5},{2,0},{3,7},{4,6},{5,1},{6,4},{7,3},{8,10},{9,13},{10,... | collective-permute-start | bytes 884744 | tf_op jit(solution)/shard_map/ppermute | solution.py:391
  108.3 8.8 %collective-permute-start.32 = (f32[16,128,128]{2,1,0:T(8,128)S(1)}, f32[16,128,128]{2,1,0:T(8,128)S(1)}, u32[]{:S(2)}, u32[]{:S(2)}) collective-permute-start(f32[16,128,128]{2,1,0:T(8,128)S(1)} %pad_maximum_fusion.refs_1_), channel_id=1, source_target_pairs={{0,1},{1,0},{2,3},{3,2},{4,5},{5,4},{6,7},{7,6},{8,9},{9,8},{10,11... | collective-permute-start | bytes 3145736 | tf_op jit(solution)/shard_map/ppermute | solution.py:391
  110.3 6.4 %collective-permute-start.21 = (f32[8,64,128]{2,1,0:T(8,128)S(1)}, f32[8,64,128]{2,1,0:T(8,128)S(1)}, u32[]{:S(2)}, u32[]{:S(2)}) collective-permute-start(f32[8,64,128]{2,1,0:T(8,128)S(1)} %pad_maximum_fusion.7), channel_id=1, source_target_pairs={{0,8},{1,3},{2,10},{3,1},{4,12},{5,7},{6,14},{7,5},{8,0},{9,11},{1... | collective-permute-start | bytes 786440 | tf_op jit(solution)/shard_map/ppermute | solution.py:391
  (19 other events, 96.5 us)
